TPU v7x, 32 devices: a whole 2x2x4 slice. The times are simulated.
32 devices in a mesh: groups: 2 (over y), wide: 4 (over x, core), narrow: 4 (over z).
Axes of the slice: x: 2, y: 2, z: 4, core: 2. Of those that a mesh axis runs over, the one named last changes fastest.
Arguments:
- basis: bfloat16 [128, 64, 2, 512], P(('groups', 'wide'), 'narrow'), parts along dimension 0, may hold values from -0.25 to 0.25
- kappa: float32 [128, 64, 2], P(('groups', 'wide'), 'narrow'), parts along dimension 0, may hold values from 0.1 to 1
- velocity: float32 [3, 512], P(None, 'groups'), parts along dimension 1, may hold values from -2 to 2
- coefficients: float32 [512, 512], P('groups'), parts along dimension 0, may hold values from -6 to 6
- propagator: float32 [1024, 512], P('groups'), parts along dimension 0, may hold values from -0.25 to 0.25
Outputs:
- advanced: float32 [512, 512], P(('groups', 'wide', 'narrow')), parts along dimension 0
There are 2 independent parts, one for each index of `groups`. A program takes and returns all parts, laid end to end along the dimension named above; each array names one. Nothing has to cross between parts.
All inputs are finite; a program needn't handle non-finite values.
Results may differ from a plain program's by a relative error of at most 0.0056.
Values may be sent and summed in bfloat16 or wider, within the bound.
A program may use at most 64 MiB of HBM per device.

v0:
```python
import functools
import math

import jax
import jax.numpy as jnp
from jax import lax
from jax.experimental import pallas as pl
from jax.experimental.pallas import tpu as pltpu
from jax.sharding import PartitionSpec as P

ITERS = 2
WIRE = jnp.bfloat16
PAD = 8

step_size = 4.0

NT = (((1,), (1,)), ((), ()))
NN = (((1,), (0,)), ((), ()))


def peer(me, offset):
    result, bit = me, 1
    while bit <= offset:
        if offset & bit:
            result = result + (1 - 2 * ((me // bit) % 2)) * bit
        bit *= 2
    return result


def dot(a, b, dims):
    return lax.dot_general(a, b, dims, preferred_element_type=jnp.float32)


def kernel(
    sizes, wide, narrow, scale,
    basis_ref, kappa_ref, velocity_ref, coefficients_ref, propagator_ref, out_ref,
    faces, halo_x, halo_y, field, forcing_ref, turned, g_high, g_low,
    pair_out, pair_in, reduced, kept, landed, gathered,
    halo_send, halo_recv, pair_send, pair_recv, r_send, r_recv, g_send, g_recv, f_send, f_recv,
):
    size_x, size_y, size_z = sizes
    rows = size_y * size_z
    samples, modes = coefficients_ref.shape
    owned = samples // (wide * narrow)
    chunk = owned * narrow
    me_w, me_n = lax.axis_index("wide"), lax.axis_index("narrow")

    halo_x[...] = jnp.zeros_like(halo_x)
    halo_y[...] = jnp.zeros_like(halo_y)
    barrier = pltpu.get_barrier_semaphore()
    greeted = [(e, 0) for e in range(1, wide)] + [(e, d) for e in range(0, wide, 2) for d in range(1, narrow)]
    for e, d in greeted:
        pl.semaphore_signal(
            barrier, inc=1, device_id={"wide": peer(me_w, e), "narrow": peer(me_n, d)},
            device_id_type=pl.DeviceIdType.MESH,
        )

    for x in range(size_x):
        at = x * rows
        faces[0, x * size_z:(x + 1) * size_z, :] = basis_ref[at:at + size_z, :]
        faces[1, x * size_z:(x + 1) * size_z, :] = basis_ref[at + rows - size_z:at + rows, :]
    g_high[...] = propagator_ref[...].astype(jnp.bfloat16)
    g_low[...] = (propagator_ref[...] - g_high[...].astype(jnp.float32)).astype(jnp.bfloat16)

    pl.semaphore_wait(barrier, len(greeted))

    def remote(src, dst, send, recv, **where):
        return pltpu.make_async_remote_copy(
            src_ref=src, dst_ref=dst, send_sem=send, recv_sem=recv,
            device_id=where, device_id_type=pl.DeviceIdType.MESH,
        )

    last = (size_x - 1) * rows
    halos = (
        (remote(faces.at[1], halo_y.at[0], halo_send.at[0], halo_recv.at[0], narrow=lax.rem(me_n + 1, narrow)),
         me_n < narrow - 1, me_n > 0),
        (remote(faces.at[0], halo_y.at[1], halo_send.at[1], halo_recv.at[1], narrow=lax.rem(me_n + narrow - 1, narrow)),
         me_n > 0, me_n < narrow - 1),
        (remote(basis_ref.at[pl.ds(last, rows)], halo_x.at[0], halo_send.at[2], halo_recv.at[2], wide=lax.rem(me_w + 1, wide)),
         me_w < wide - 1, me_w > 0),
        (remote(basis_ref.at[pl.ds(0, rows)], halo_x.at[1], halo_send.at[3], halo_recv.at[3], wide=lax.rem(me_w + wide - 1, wide)),
         me_w > 0, me_w < wide - 1),
    )
    for copy, sends, receives in halos:
        pl.when(sends)(copy.start)

    z_index = lax.broadcasted_iota(jnp.int32, (rows, samples), 0) % size_z
    first_row = (me_w * narrow + me_n) * owned
    if owned % 8 == 0:
        first_row = pl.multiple_of(first_row, 8)
    state = coefficients_ref[pl.ds(first_row, owned), :]
    lift_rows = coefficients_ref[...].astype(jnp.bfloat16)
    pending = []

    def lifted(of):
        return dot(of, lift_rows, NT).astype(jnp.bfloat16).astype(jnp.float32)

    for step in range(ITERS):
        field[1:size_x + 1, PAD:PAD + rows, :] = lifted(basis_ref[...]).reshape(size_x, rows, samples)
        if step == 0:
            for copy, sends, receives in halos:
                pl.when(receives)(copy.wait_recv)
        field[0, PAD:PAD + rows, :] = lifted(halo_x[0])
        field[size_x + 1, PAD:PAD + rows, :] = lifted(halo_x[1])
        before, after = lifted(halo_y[0]), lifted(halo_y[1])
        for x in range(size_x):
            field[x + 1, PAD - size_z:PAD, :] = before[x * size_z:(x + 1) * size_z]
            field[x + 1, PAD + rows:PAD + rows + size_z, :] = after[x * size_z:(x + 1) * size_z]

        def slab(x, carry):
            center = field[x + 1, PAD:PAD + rows, :]
            x_next = field[x + 2, PAD:PAD + rows, :]
            x_prev = field[x, PAD:PAD + rows, :]
            y_next = field[x + 1, PAD + size_z:PAD + rows + size_z, :]
            y_prev = field[x + 1, PAD - size_z:PAD + rows - size_z, :]
            z_next = jnp.where(z_index < size_z - 1, field[x + 1, PAD + 1:PAD + rows + 1, :], 0.0)
            z_prev = jnp.where(z_index > 0, field[x + 1, PAD - 1:PAD + rows - 1, :], 0.0)
            spread = x_next + x_prev + y_next + y_prev + z_next + z_prev - 6.0 * center
            carried = velocity_ref[0:1, :] * (x_next * x_next - x_prev * x_prev)
            carried = carried + velocity_ref[1:2, :] * (y_next * y_next - y_prev * y_prev)
            carried = carried + velocity_ref[2:3, :] * (z_next * z_next - z_prev * z_prev)
            at = pl.multiple_of(x * rows, rows)
            result = kappa_ref[pl.ds(at, rows), :] * spread - 0.25 * carried
            forcing_ref[pl.ds(at, rows), :] = result.astype(jnp.bfloat16)
            return carry

        lax.fori_loop(0, size_x, slab, 0, unroll=4)
        turned[...] = forcing_ref[...].T

        def projected(target):
            at = pl.multiple_of(target * chunk, chunk)
            return dot(turned[pl.ds(at, chunk), :], basis_ref[...], NN)

        pairs = []
        for i in reversed(range(wide // 2)):
            pair_out[step, i] = projected(peer(me_w, 2 * i + 1))
            copy = remote(
                pair_out.at[step, i], pair_in.at[step, i], pair_send.at[step, i], pair_recv.at[step, i],
                wide=peer(me_w, 1),
            )
            copy.start()
            pairs.append((i, copy))
        totals = [projected(peer(me_w, 2 * i)) for i, copy in pairs]
        spread_out = []
        for (i, copy), total in zip(pairs, totals):
            copy.wait_recv()
            pending.append(copy)
            total = total + pair_in[step, i]
            for n in range(narrow):
                block = total[n * owned:(n + 1) * owned]
                reduced[step, i, n] = block.astype(WIRE)
                if i == 0:
                    kept[n] = block
            for d in reversed(range(narrow)):
                if i == 0 and d == 0:
                    continue
                copy = remote(
                    reduced.at[step, i, peer(me_n, d)], landed.at[step, i, d],
                    r_send.at[step, i, d], r_recv.at[step, i, d],
                    wide=peer(me_w, 2 * i), narrow=peer(me_n, d),
                )
                copy.start()
                spread_out.append((i, d, copy))
        summed = kept[me_n]
        for i, d, copy in reversed(spread_out):
            copy.wait_recv()
            pending.append(copy)
            summed = summed + landed[step, i, d].astype(jnp.float32)

        update = state + step_size * (summed * scale)
        high = update.astype(jnp.bfloat16)
        low = (update - high.astype(jnp.float32)).astype(jnp.bfloat16)
        small = dot(high, g_low[...], NT) + dot(low, g_high[...], NT)
        state = update + (dot(high, g_high[...], NT) + small)

        if step + 1 < ITERS:
            gathered[step, me_w, me_n] = state.astype(jnp.bfloat16)
            others = [(i, d) for d in range(narrow) for i in range(wide // 2) if i + d > 0]
            direct, inside = {}, []
            own = gathered.at[step, me_w, me_n]
            for i, d in reversed(others):
                direct[i, d] = remote(
                    own, own, g_send.at[step, i, d], g_recv.at[step, i, d],
                    wide=peer(me_w, 2 * i), narrow=peer(me_n, d),
                )
                direct[i, d].start()

            def beside(i, d):
                block = gathered.at[step, peer(me_w, 2 * i), peer(me_n, d)]
                copy = remote(block, block, f_send.at[step, i, d], f_recv.at[step, i, d], wide=peer(me_w, 1))
                copy.start()
                inside.append(copy)

            beside(0, 0)
            for i, d in others:
                direct[i, d].wait_recv()
                pending.append(direct[i, d])
                beside(i, d)
            for copy in inside:
                copy.wait_recv()
                pending.append(copy)
            lift_rows = gathered[step].reshape(samples, modes)

    out_ref[...] = state
    for copy in pending:
        copy.wait_send()
    for copy, sends, receives in halos:
        pl.when(sends)(copy.wait_send)


def body(basis, kappa, velocity, coefficients, propagator):
    size_x, size_y, size_z, modes = basis.shape
    samples = coefficients.shape[0]
    wide, narrow = lax.axis_size("wide"), lax.axis_size("narrow")
    owned = samples // (wide * narrow)
    chunk = owned * narrow
    cells, rows = size_x * size_y * size_z, size_y * size_z
    scale = 1.0 / math.sqrt(cells * wide * narrow)
    f32, bf16 = jnp.float32, jnp.bfloat16
    dma = pltpu.SemaphoreType.DMA
    vmem = pl.BlockSpec(memory_space=pltpu.VMEM)
    return pl.pallas_call(
        functools.partial(kernel, (size_x, size_y, size_z), wide, narrow, scale),
        out_shape=jax.ShapeDtypeStruct((owned, modes), f32),
        in_specs=[vmem] * 5,
        out_specs=vmem,
        scratch_shapes=[
            pltpu.VMEM((2, size_x * size_z, modes), bf16),
            pltpu.VMEM((2, rows, modes), bf16),
            pltpu.VMEM((2, size_x * size_z, modes), bf16),
            pltpu.VMEM((size_x + 2, rows + 2 * PAD, samples), f32),
            pltpu.VMEM((cells, samples), bf16),
            pltpu.VMEM((samples, cells), bf16),
            pltpu.VMEM((modes, modes), bf16),
            pltpu.VMEM((modes, modes), bf16),
            pltpu.VMEM((ITERS, wide // 2, chunk, modes), f32),
            pltpu.VMEM((ITERS, wide // 2, chunk, modes), f32),
            pltpu.VMEM((ITERS, wide // 2, narrow, owned, modes), WIRE),
            pltpu.VMEM((narrow, owned, modes), f32),
            pltpu.VMEM((ITERS, wide // 2, narrow, owned, modes), WIRE),
            pltpu.VMEM((ITERS - 1, wide, narrow, owned, modes), bf16),
            dma((4,)), dma((4,)),
            dma((ITERS, wide // 2)), dma((ITERS, wide // 2)),
            dma((ITERS, wide // 2, narrow)), dma((ITERS, wide // 2, narrow)),
            dma((ITERS - 1, wide // 2, narrow)), dma((ITERS - 1, wide // 2, narrow)),
            dma((ITERS - 1, wide // 2, narrow)), dma((ITERS - 1, wide // 2, narrow)),
        ],
        compiler_params=pltpu.CompilerParams(
            collective_id=0, has_side_effects=True, vmem_limit_bytes=48 * 1024 * 1024
        ),
    )(basis.reshape(cells, modes), kappa.reshape(cells, 1), velocity, coefficients, propagator)


def solution(mesh):
    placed = (
        P(("groups", "wide"), "narrow", None, None),
        P(("groups", "wide"), "narrow", None),
        P(None, "groups"),
        P("groups", None),
        P("groups", None),
    )
    return jax.shard_map(
        body,
        mesh=mesh,
        in_specs=placed,
        out_specs=P(("groups", "wide", "narrow"), None),
        check_vma=False,
    )
```

profile of v0, /device:TPU:0, one launch (start us, length us, event | category | flops | bytes accessed | tf_op | source)
XLA Modules:
  0.0 34.5 jit_solution(9242371018261072477)
XLA Ops:
  0.0 0.0 copy-start
  0.0 1.0 %copy.7 = f32[16,16,2]{2,1,0:T(8,128)S(1)} copy(f32[16,16,2]{1,2,0:T(2,128)} %param.6) | data formatting | bytes 4096 | tf_op args[1]
  1.0 0.1 reshape.8.kappa_ref
  1.1 0.0 copy-start.1
  1.1 0.0 copy-start.2
  1.1 1.3 %reshape.6.basis_ref = bf16[512,512]{1,0:T(8,128)(2,1)S(1)} reshape(bf16[16,16,2,512]{3,2,1,0:T(2,128)(2,1)} %param.5) | data formatting | bytes 1048576 | tf_op jit(solution)/shard_map/reshape | solution.py:251
  2.4 0.0 copy-done
  2.4 0.0 copy-done.1
  2.4 0.0 copy-done.2
  2.4 31.4 %shard_map.55 = f32[16,512]{1,0:T(8,128)S(1)} custom-call(bf16[512,512]{1,0:T(8,128)(2,1)S(1)} %reshape.6.basis_ref, f32[512,1]{1,0:T(8,128)S(1)} %reshape.8.kappa_ref, f32[3,256]{1,0:T(4,128)S(1)} %copy-done.2, f32[256,512]{1,0:T(8,128)S(1)} %copy-done.1, f32[512,512]{1,0:T(8,128)S(1)} %copy-done), custom_call_target="tpu_custom_call" | custom-call | tf_op jit(solution)/shard_map/pallas_call | solution.py:222
  33.9 0.6 %copy.10 = f32[16,512]{1,0:T(8,128)} copy(f32[16,512]{1,0:T(8,128)S(1)} %shard_map.55) | data formatting | bytes 65536
Async XLA Ops:
  0.0 2.4 %copy-start = (f32[512,512]{1,0:T(8,128)S(1)}, f32[512,512]{1,0:T(8,128)}, u32[]{:S(2)}) copy-start(f32[512,512]{1,0:T(8,128)} %propagator_ref.1) | copy-start | bytes 3145732
  1.1 1.3 %copy-start.1 = (f32[256,512]{1,0:T(8,128)S(1)}, f32[256,512]{1,0:T(8,128)}, u32[]{:S(2)}) copy-start(f32[256,512]{1,0:T(8,128)} %coefficients_ref.1) | copy-start | bytes 1572868
  1.1 1.3 %copy-start.2 = (f32[3,256]{1,0:T(4,128)S(1)}, f32[3,256]{1,0:T(4,128)}, u32[]{:S(2)}) copy-start(f32[3,256]{1,0:T(4,128)} %velocity_ref.1) | copy-start | bytes 9220
where the time goes:
time: 34.7 us; the launch traced here: 34.5 us
  Pallas kernels  31.4 us (90%)
  local copies, waits for them, and re-layouts  3 us (9%)
    pallas_call x1, Pallas kernels, body(): pl.pallas_call(functools.partial(kernel, (size_x, size_y, size_z), wide,...  31.4 us
    unnamed x8, local copies, waits for them, and re-layouts  1.6 us
    reshape x1, local copies, waits for them, and re-layouts, body(): basis.reshape(cells, modes)  1.3 us

commit v1 on v0

v1 whole, which is shorter than its diff:
```python
import functools
import math

import jax
import jax.numpy as jnp
from jax import lax
from jax.experimental import pallas as pl
from jax.experimental.pallas import tpu as pltpu
from jax.sharding import PartitionSpec as P

ITERS = 2
WIRE = jnp.bfloat16
LANES = 128
CORES = 2

step_size = 4.0

NT = (((1,), (1,)), ((), ()))
NN = (((1,), (0,)), ((), ()))
f32, bf16 = jnp.float32, jnp.bfloat16


def peer(me, offset):
    result, bit = me, 1
    while bit <= offset:
        if offset & bit:
            result = result + (1 - 2 * ((me // bit) % 2)) * bit
        bit *= 2
    return result


def dot(a, b, dims):
    return lax.dot_general(a, b, dims, preferred_element_type=f32)


def kernel(
    chips, narrow, scale,
    basis_hbm, kappa_hbm, velocity_hbm, coefficients_hbm, propagator_hbm, out_ref,
    basis, border, kappa, velocity, coefficients, propagator,
    field, factor, speed, g_high, g_low,
    reduced, landed, kept, mine, gathered,
    load_sem, mate_send, mate_recv, y_send, y_recv, x_send, x_recv,
    r_send, r_recv, g_send, g_recv,
):
    size_x, size_y, size_z, modes = basis_hbm.shape
    slices, depth = basis.shape[:2]
    owned = coefficients.shape[2]
    samples = velocity.shape[1]
    unit = chips * owned
    pitch = size_y * size_z
    half, cells = size_x * pitch, depth * pitch
    tiles = cells // LANES
    x_rows, y_rows = size_y, depth
    y_base = border.shape[1] - 2 * y_rows
    x_base = (y_base - x_rows, 0)
    wide = chips * CORES
    me_w, me_n = lax.axis_index("wide"), lax.axis_index("narrow")
    chip, core = me_w // CORES, me_w % CORES

    def lanes_of(ct):
        return pl.ds(ct * LANES, LANES)

    barrier = pltpu.get_barrier_semaphore()
    greeted = [(e, d) for d in range(narrow) for e in range(wide) if e + d > 0]
    for e, d in greeted:
        pl.semaphore_signal(
            barrier, inc=1, device_id={"wide": peer(me_w, e), "narrow": peer(me_n, d)},
            device_id_type=pl.DeviceIdType.MESH,
        )
    mine_x, theirs_x = pl.ds(core * size_x, size_x), pl.ds((1 - core) * size_x, size_x)
    loads = [
        pltpu.make_async_copy(basis_hbm.at[:, :, :, lanes_of(ct)], basis.at[ct, mine_x], load_sem.at[0])
        for ct in range(slices)
    ]
    for load in loads:
        load.start()
    starts = [
        pltpu.make_async_copy(coefficients_hbm.at[CORES * x + core], coefficients.at[x], load_sem.at[3 + x])
        for x in range(chips)
    ]
    for start in starts:
        start.start()
    own_kappa = pltpu.make_async_copy(kappa_hbm, kappa.at[core], load_sem.at[1])
    own_kappa.start()
    speeds = pltpu.make_async_copy(velocity_hbm, velocity, load_sem.at[2])
    speeds.start()
    inverse = pltpu.make_async_copy(propagator_hbm, propagator, load_sem.at[3 + chips])
    inverse.start()

    def clear(first, count):
        border[:, pl.ds(first, count)] = jnp.zeros((slices, count) + border.shape[2:], bf16)

    pl.when(chip == 0)(lambda: clear(x_base[0], x_rows))
    pl.when(chip == chips - 1)(lambda: clear(x_base[1], x_rows))
    pl.when(me_n == 0)(lambda: clear(y_base, y_rows))
    pl.when(me_n == narrow - 1)(lambda: clear(y_base + y_rows, y_rows))

    pl.semaphore_wait(barrier, len(greeted))

    def remote(src, dst, send, recv, w, n):
        return pltpu.make_async_remote_copy(
            src_ref=src, dst_ref=dst, send_sem=send, recv_sem=recv,
            device_id={"wide": w, "narrow": n}, device_id_type=pl.DeviceIdType.MESH,
        )

    def arrival(ref, send, recv):
        return remote(ref, ref, send, recv, me_w, me_n)

    faces = []
    for j, (from_y, step) in enumerate(((size_y - 1, 1), (0, -1))):
        n = lax.rem(me_n + step + narrow, narrow)
        sends = jnp.logical_and(me_n + step >= 0, me_n + step < narrow)
        receives = jnp.logical_and(me_n - step >= 0, me_n - step < narrow)
        put = pl.ds(y_base + j * y_rows + core * size_x, size_x)
        for k in range(CORES):
            source = core if k == 0 else 1 - core
            came = border.at[:, pl.ds(y_base + j * y_rows + source * size_x, size_x)]
            parts = [
                remote(
                    basis_hbm.at[:, from_y, :, lanes_of(ct)], border.at[ct, put],
                    y_send.at[j, k], y_recv.at[j, k], peer(me_w, k), n,
                )
                for ct in range(slices)
            ]
            faces.append((
                parts, sends, arrival(came, y_send.at[j, k], y_recv.at[j, k]), receives,
            ))
    toward = chip + 2 * core - 1
    x_to = lax.rem(toward + chips, chips)
    sends = jnp.logical_and(toward >= 0, toward < chips)
    put = pl.ds((1 - core) * x_base[1] + core * x_base[0], x_rows)
    if x_base[1] == 0:
        put = pl.ds(core * x_base[0], x_rows)
    for k in range(CORES):
        parts = [
            remote(
                basis_hbm.at[core * (size_x - 1), :, :, lanes_of(ct)], border.at[ct, put],
                x_send.at[k], x_recv.at[core], CORES * x_to + k, me_n,
            )
            for ct in range(slices)
        ]
        came = border.at[:, pl.ds(x_base[1 - k], x_rows)]
        receives = chip < chips - 1 if k == 0 else chip > 0
        faces.append((parts, sends, arrival(came, x_send.at[k], x_recv.at[k]), receives))
    for parts, sends, back, receives in faces:
        def go(parts=parts):
            for part in parts:
                part.start()
        pl.when(sends)(go)
    mate = [
        remote(
            basis_hbm.at[:, :, :, lanes_of(ct)], basis.at[ct, mine_x],
            mate_send.at[0], mate_recv.at[0], peer(me_w, 1), me_n,
        )
        for ct in range(slices)
    ]
    for part in mate:
        part.start()
    mate_back = arrival(basis.at[:, theirs_x], mate_send.at[0], mate_recv.at[0])
    mate_kappa = remote(kappa_hbm, kappa.at[core], mate_send.at[1], mate_recv.at[1], peer(me_w, 1), me_n)
    mate_kappa.start()

    for load in loads:
        load.wait()
    for start in starts:
        start.wait()
    first_rows = jnp.concatenate([
        coefficients[peer(chip, e), peer(me_n, d)].astype(bf16) for d in range(narrow) for e in range(chips)
    ], axis=0)

    def rounded(rows, against):
        return dot(rows, against, NT).astype(bf16).astype(f32)

    def half_of(at):
        return jnp.concatenate([basis[ct, at].reshape(half, LANES) for ct in range(slices)], axis=1)

    def all_cells():
        return jnp.concatenate([basis[ct].reshape(cells, LANES) for ct in range(slices)], axis=1)

    def border_cells():
        return jnp.concatenate(
            [border[ct].reshape(border.shape[1] * size_z, LANES) for ct in range(slices)], axis=1
        )

    outer = pl.ds(cells, border.shape[1] * size_z)
    field[:, pl.ds(pl.multiple_of(core * half, LANES), half)] = rounded(first_rows, half_of(mine_x))

    speeds.wait()
    for k in range(3):
        speed[k] = (0.25 * jnp.broadcast_to(velocity[k:k + 1, :], (LANES, samples))).T

    cell = lax.broadcasted_iota(jnp.int32, (1, cells), 1)
    y_of, z_of = (cell % pitch) // size_z, cell % size_z
    pick = (y_of == lax.broadcasted_iota(jnp.int32, (size_y, cells), 0)).astype(bf16)
    line = lax.broadcasted_iota(jnp.int32, (depth * size_z, cells), 0)
    own_row = (line == (cell // pitch) * size_z + z_of).astype(f32)
    own_kappa.wait()
    mate_kappa.wait_recv()
    rest = kappa[...].reshape(depth * size_z, size_y)
    found = jnp.zeros((depth * size_z, cells), f32)
    for _ in range(3):
        part = rest.astype(bf16)
        rest = rest - part.astype(f32)
        found = found + dot(part, pick, NN)
    factor[...] = jnp.broadcast_to(jnp.sum(found * own_row, axis=0, keepdims=True), factor.shape)

    mate_back.wait_recv()
    field[:, pl.ds(pl.multiple_of((1 - core) * half, LANES), half)] = rounded(first_rows, half_of(theirs_x))
    for parts, sends, back, receives in faces:
        pl.when(receives)(back.wait_recv)
    field[:, outer] = rounded(first_rows, border_cells())

    lane = lax.broadcasted_iota(jnp.int32, (8, LANES), 1)
    lane_x, lane_y, lane_z = lane // pitch, (lane % pitch) // size_z, lane % size_z
    per_tile = LANES // pitch
    low_y, high_y = lane_y == 0, lane_y == size_y - 1
    first_of_tile, last_of_tile = lane < pitch, lane >= LANES - pitch
    from_border = lane_x * size_z + lane_z + jnp.where(high_y, y_rows * size_z, 0)
    z_sign = jnp.where(lane_z == 0, 1.0, -1.0)

    def stencil(first, speeds_of):
        def at(t):
            return field[first:first + 8, t * LANES:(t + 1) * LANES]

        def turn(value, by):
            return pltpu.roll(value, by % LANES, 1)

        v_x, v_y, v_z = speeds_of
        if size_z == 2:
            v_z = v_z * z_sign
        center = [at(t) for t in range(tiles + 1)]
        ahead = [turn(value, -pitch) for value in center]
        behind = [turn(value, pitch) for value in center]
        y_border = at(tiles + 1)
        out = []
        for t in range(tiles):
            mid = center[t]
            x_next = jnp.where(last_of_tile, ahead[t + 1], ahead[t])
            x_prev = jnp.where(first_of_tile, behind[t - 1], behind[t])
            outside = jnp.take_along_axis(y_border, from_border + t * per_tile * size_z, axis=1)
            y_next = jnp.where(high_y, outside, turn(mid, -size_z))
            y_prev = jnp.where(low_y, outside, turn(mid, size_z))
            x_sum, y_sum = x_next + x_prev, y_next + y_prev
            carried = v_x * (x_sum * (x_next - x_prev)) + v_y * (y_sum * (y_next - y_prev))
            if size_z == 2:
                z_sum = jnp.where(lane_z == 0, turn(mid, -1), turn(mid, 1))
                carried = carried + v_z * (z_sum * z_sum)
            else:
                z_next = jnp.where(lane_z < size_z - 1, turn(mid, -1), 0.0)
                z_prev = jnp.where(lane_z > 0, turn(mid, 1), 0.0)
                z_sum = z_next + z_prev
                carried = carried + v_z * (z_sum * (z_next - z_prev))
            spread = x_sum + y_sum + z_sum - 6.0 * mid
            out.append(factor[:, t * LANES:(t + 1) * LANES] * spread - carried)
        return jnp.concatenate(out, axis=1)

    def speeds_at(d, g):
        pieces = [[], [], []]
        for r in range(8 * g, 8 * g + 8, min(8, owned)):
            e, inner = r // owned, r % owned
            row = ((CORES * peer(chip, e) + core) * narrow + peer(me_n, d)) * owned + inner
            count = min(8, owned)
            if count % 8 == 0:
                row = pl.multiple_of(row, 8)
            for k in range(3):
                pieces[k].append(speed[k, pl.ds(row, count), :])
        return [jnp.concatenate(p, axis=0) if len(p) > 1 else p[0] for p in pieces]

    def scatter(d, waits):
        forcing = jnp.concatenate(
            [stencil(d * unit + 8 * g, speeds_at(d, g)) for g in range(unit // 8)], axis=0
        ).astype(bf16)
        total = dot(forcing, all_cells(), NN)
        for e in reversed(range(chips)):
            block = total[e * owned:(e + 1) * owned]
            if d + e == 0:
                kept[...] = block
                continue
            copy = remote(
                reduced.at[d, e], landed.at[d, e], r_send.at[d, e], r_recv.at[d, e],
                CORES * peer(chip, e) + core, peer(me_n, d),
            )
            if waits:
                copy.wait_send()
            reduced[d, e] = block.astype(WIRE)
            copy.start()

    def all_sends(ref, sends, recvs):
        for d in range(narrow):
            for e in range(chips):
                if d + e > 0:
                    arrival(ref(d, e), sends.at[d, e], recvs.at[d, e]).wait_send()

    state = coefficients[chip, me_n]
    for step in range(ITERS):
        for d in range(narrow) if step else reversed(range(narrow)):
            if step > 0:
                blocks = []
                for e in range(chips):
                    if d + e == 0:
                        blocks.append(mine[...])
                    else:
                        arrival(gathered.at[d, e], g_send.at[d, e], g_recv.at[d, e]).wait_recv()
                        blocks.append(gathered[d, e])
                rows = jnp.concatenate(blocks, axis=0)
                field[d * unit:(d + 1) * unit, :cells] = rounded(rows, all_cells())
                field[d * unit:(d + 1) * unit, outer] = rounded(rows, border_cells())
            scatter(d, step > 0)

        if step == 0:
            inverse.wait()
            high = propagator[...].astype(bf16)
            g_high[...] = high.T
            g_low[...] = (propagator[...] - high.astype(f32)).astype(bf16).T

        summed = kept[...]
        for d in range(narrow):
            for e in range(chips):
                if d + e > 0:
                    arrival(landed.at[d, e], r_send.at[d, e], r_recv.at[d, e]).wait_recv()
                    summed = summed + landed[d, e].astype(f32)

        update = state + step_size * (summed * scale)
        high = update.astype(bf16)
        low = (update - high.astype(f32)).astype(bf16)
        both = dot(jnp.concatenate([high, low], axis=0), g_high[...], NN)
        small = both[owned:] + dot(high, g_low[...], NN)
        state = update + (both[:owned] + small)

        if step + 1 < ITERS:
            if step > 0:
                all_sends(lambda d, e: mine, g_send, g_recv)
            mine[...] = state.astype(bf16)
            for d in reversed(range(narrow)):
                for e in reversed(range(chips)):
                    if d + e > 0:
                        remote(
                            mine, gathered.at[d, e], g_send.at[d, e], g_recv.at[d, e],
                            CORES * peer(chip, e) + core, peer(me_n, d),
                        ).start()

    out_ref[...] = state
    all_sends(lambda d, e: reduced.at[d, e], r_send, r_recv)
    all_sends(lambda d, e: mine, g_send, g_recv)
    for parts, sends, back, receives in faces:
        def sent(parts=parts):
            for part in parts:
                part.wait_send()
        pl.when(sends)(sent)
    for part in mate:
        part.wait_send()
    mate_kappa.wait_send()


def body(basis, kappa, velocity, coefficients, propagator):
    size_x, size_y, size_z, modes = basis.shape
    samples = coefficients.shape[0]
    wide, narrow = lax.axis_size("wide"), lax.axis_size("narrow")
    chips = wide // CORES
    owned = samples // (wide * narrow)
    unit = chips * owned
    scale = 1.0 / math.sqrt(size_x * size_y * size_z * wide * narrow)
    pitch = size_y * size_z
    depth = CORES * size_x
    cells = depth * pitch
    assert LANES % pitch == 0 and cells % LANES == 0 and 2 * pitch <= LANES
    assert 2 * depth * size_z == LANES and unit % 8 == 0
    border = 2 * LANES // size_z
    dma = pltpu.SemaphoreType.DMA
    hbm = pl.BlockSpec(memory_space=pltpu.HBM)
    inputs = (
        basis, kappa.transpose(0, 2, 1), velocity,
        coefficients.reshape(wide, narrow, owned, modes), propagator,
    )
    return pl.pallas_call(
        functools.partial(kernel, chips, narrow, scale),
        out_shape=jax.ShapeDtypeStruct((owned, modes), f32),
        in_specs=[hbm] * len(inputs),
        out_specs=pl.BlockSpec(memory_space=pltpu.VMEM),
        scratch_shapes=[
            pltpu.VMEM((modes // LANES, depth, size_y, size_z, LANES), bf16),
            pltpu.VMEM((modes // LANES, border, size_z, LANES), bf16),
            pltpu.VMEM((CORES, size_x, size_z, size_y), f32),
            pltpu.VMEM((3, samples), f32),
            pltpu.VMEM((chips, narrow, owned, modes), f32),
            pltpu.VMEM((modes, modes), f32),
            pltpu.VMEM((narrow * unit, cells + border * size_z), f32),
            pltpu.VMEM((8, cells), f32),
            pltpu.VMEM((3, samples, LANES), f32),
            pltpu.VMEM((modes, modes), bf16),
            pltpu.VMEM((modes, modes), bf16),
            pltpu.VMEM((narrow, chips, owned, modes), WIRE),
            pltpu.VMEM((narrow, chips, owned, modes), WIRE),
            pltpu.VMEM((owned, modes), f32),
            pltpu.VMEM((owned, modes), bf16),
            pltpu.VMEM((narrow, chips, owned, modes), bf16),
            dma((4 + chips,)), dma((2,)), dma((2,)),
            dma((2, CORES)), dma((2, CORES)), dma((CORES,)), dma((CORES,)),
            dma((narrow, chips)), dma((narrow, chips)),
            dma((narrow, chips)), dma((narrow, chips)),
        ],
        compiler_params=pltpu.CompilerParams(
            collective_id=0, has_side_effects=True, vmem_limit_bytes=48 * 1024 * 1024
        ),
    )(*(pltpu.with_memory_space_constraint(value, pltpu.HBM) for value in inputs))


def solution(mesh):
    placed = (
        P(("groups", "wide"), "narrow", None, None),
        P(("groups", "wide"), "narrow", None),
        P(None, "groups"),
        P("groups", None),
        P("groups", None),
    )
    return jax.shard_map(
        body,
        mesh=mesh,
        in_specs=placed,
        out_specs=P(("groups", "wide", "narrow"), None),
        check_vma=False,
    )
```

time: 34.7 us -> 30.1 us (0.87)
  local copies, waits for them, and re-layouts: 3 us -> 0.62 us
  Pallas kernels: 31.4 us -> 29.3 us
    pallas_call x1, Pallas kernels: 31.4 us -> 29.3 us  [body(): pl.pallas_call(functools.partial(kernel, chips, narrow, scale), out_shape...]
    reshape x2 -> x0, local copies, waits for them, and re-layouts: 1.39 us -> none  [the longest x1 1.3 us: body(): basis.reshape(cells, modes)]
    unnamed x8 -> x1, local copies, waits for them, and re-layouts: 1.6 us -> 0.62 us
where the time goes in v1:
time: 30.1 us; the launch traced here: 29.9 us
  Pallas kernels  29.3 us (97%)
  local copies, waits for them, and re-layouts  0.62 us (2%)
    pallas_call x1, Pallas kernels, body(): pl.pallas_call(functools.partial(kernel, chips, narrow, scale), out_shape...  29.3 us
    unnamed x1, local copies, waits for them, and re-layouts  0.62 us

profile of v1, /device:TPU:0, one launch (start us, length us, event | category | flops | bytes accessed | tf_op | source)
XLA Modules:
  0.0 29.9 jit_solution(13293212121148218201)
XLA Ops:
  0.0 29.3 %shard_map.55 = f32[16,512]{1,0:T(8,128)S(1)} custom-call(bf16[16,16,2,512]{3,2,1,0:T(2,128)(2,1)} %basis_hbm.1, f32[16,2,16]{2,1,0:T(2,128)} %bitcast.3, f32[3,256]{1,0:T(4,128)} %velocity_hbm.1, f32[4,4,16,512]{3,2,1,0:T(8,128)} %bitcast.2, f32[512,512]{1,0:T(8,128)} %propagator_hbm.1), custom_call_target="tpu_custom_call" | custom-call | tf_op jit(solution)/shard_map/pallas_call | solution.py:375
  29.3 0.6 %copy.7 = f32[16,512]{1,0:T(8,128)} copy(f32[16,512]{1,0:T(8,128)S(1)} %shard_map.55) | data formatting | bytes 65536

commit v2 on v1

v2 whole, which is shorter than its diff:
```python
import functools
import math

import jax
import jax.numpy as jnp
from jax import lax
from jax.experimental import pallas as pl
from jax.experimental.pallas import tpu as pltpu
from jax.sharding import PartitionSpec as P

ITERS = 2
WIRE = jnp.bfloat16
LANES = 128
CORES = 2

step_size = 4.0

NT = (((1,), (1,)), ((), ()))
NN = (((1,), (0,)), ((), ()))
f32, bf16 = jnp.float32, jnp.bfloat16


def peer(me, offset):
    result, bit = me, 1
    while bit <= offset:
        if offset & bit:
            result = result + (1 - 2 * ((me // bit) % 2)) * bit
        bit *= 2
    return result


def dot(a, b, dims):
    return lax.dot_general(a, b, dims, preferred_element_type=f32)


def kernel(
    chips, narrow, scale,
    basis_hbm, kappa_hbm, velocity_hbm, coefficients_hbm, propagator_hbm, out_ref,
    basis, border, kappa, velocity, coefficients, propagator,
    rows_of, columns_of, field, factor, speed, g_high, g_low,
    reduced, landed, kept, mine, gathered,
    load_sem, mate_recv, face_recv, out_send,
    r_send, r_recv, g_send, g_recv, word,
):
    size_x, size_y, size_z, modes = basis_hbm.shape
    slices, depth = basis.shape[:2]
    owned = coefficients.shape[2]
    samples = velocity.shape[1]
    unit = chips * owned
    pitch = size_y * size_z
    half, cells = size_x * pitch, depth * pitch
    tiles = cells // LANES
    x_rows, y_rows = size_y, depth
    y_base = border.shape[1] - 2 * y_rows
    x_base = (y_base - x_rows, 0)
    wide = chips * CORES
    me_w, me_n = lax.axis_index("wide"), lax.axis_index("narrow")
    chip, core = me_w // CORES, me_w % CORES

    def lanes_of(ct):
        return pl.ds(ct * LANES, LANES)

    barrier = pltpu.get_barrier_semaphore()

    def greet(w, n):
        pl.semaphore_signal(
            barrier, inc=1, device_id={"wide": w, "narrow": n}, device_id_type=pl.DeviceIdType.MESH
        )

    greet(peer(me_w, 1), me_n)
    greetings = 1
    for step in (-1, 1):
        n, x = me_n + step, chip + step
        n_there = jnp.logical_and(n >= 0, n < narrow)
        x_there = jnp.logical_and(x >= 0, x < chips)

        def along_narrow(n=n):
            for k in range(CORES):
                greet(peer(me_w, k), n)

        def along_wide(x=x):
            for k in range(CORES):
                greet(CORES * x + k, me_n)

        pl.when(n_there)(along_narrow)
        pl.when(x_there)(along_wide)
        greetings = greetings + CORES * (jnp.where(n_there, 1, 0) + jnp.where(x_there, 1, 0))
    mine_x, theirs_x = pl.ds(core * size_x, size_x), pl.ds((1 - core) * size_x, size_x)
    loads = [
        pltpu.make_async_copy(basis_hbm.at[:, :, :, lanes_of(ct)], basis.at[ct, mine_x], load_sem.at[0])
        for ct in range(slices)
    ]
    loaded = pltpu.make_async_copy(basis.at[:, mine_x], basis.at[:, mine_x], load_sem.at[0])
    for load in loads:
        load.start()
    starts = [
        pltpu.make_async_copy(coefficients_hbm.at[CORES * x + core], coefficients.at[x], load_sem.at[3])
        for x in range(chips)
    ]
    started = pltpu.make_async_copy(coefficients, coefficients, load_sem.at[3])
    for start in starts:
        start.start()
    own_kappa = pltpu.make_async_copy(kappa_hbm, kappa.at[core], load_sem.at[1])
    own_kappa.start()
    speeds = pltpu.make_async_copy(velocity_hbm, velocity, load_sem.at[4])
    speeds.start()
    inverse = pltpu.make_async_copy(propagator_hbm, propagator, load_sem.at[2])
    inverse.start()

    def clear(first, count):
        border[:, pl.ds(first, count)] = jnp.zeros((slices, count) + border.shape[2:], bf16)

    pl.when(chip == 0)(lambda: clear(x_base[0], x_rows))
    pl.when(chip == chips - 1)(lambda: clear(x_base[1], x_rows))
    pl.when(me_n == 0)(lambda: clear(y_base, y_rows))
    pl.when(me_n == narrow - 1)(lambda: clear(y_base + y_rows, y_rows))

    pl.semaphore_wait(barrier, greetings)

    def lines(count, at, where, forth, back):
        def tell(sem, step):
            pl.semaphore_signal(
                sem, inc=1, device_id=where(at + step), device_id_type=pl.DeviceIdType.MESH
            )

        def begin():
            pl.when(at == 0)(lambda: tell(forth, 1))
            pl.when(at == count - 1)(lambda: tell(back, -1))

        def go_on():
            @pl.when(jnp.logical_and(at > 0, at < count - 1))
            def _():
                pl.semaphore_wait(forth, 1)
                tell(forth, 1)
                pl.semaphore_wait(back, 1)
                tell(back, -1)

        def end():
            pl.when(at == count - 1)(lambda: pl.semaphore_wait(forth, 1))
            pl.when(at == 0)(lambda: pl.semaphore_wait(back, 1))

        return begin, go_on, end

    if chips > 2:
        for phase in lines(
            chips, chip, lambda x: {"wide": CORES * x + core, "narrow": me_n}, word.at[2], word.at[3]
        ):
            phase()
    all_in_begin, all_in_go_on, all_in = lines(
        narrow, me_n, lambda n: {"wide": me_w, "narrow": n}, word.at[0], word.at[1]
    )
    all_in_begin()

    def remote(src, dst, send, recv, w, n):
        return pltpu.make_async_remote_copy(
            src_ref=src, dst_ref=dst, send_sem=send, recv_sem=recv,
            device_id={"wide": w, "narrow": n}, device_id_type=pl.DeviceIdType.MESH,
        )

    def arrival(ref, send, recv):
        return remote(ref, ref, send, recv, me_w, me_n)

    faces = []
    for j, (from_y, step) in enumerate(((size_y - 1, 1), (0, -1))):
        n = lax.rem(me_n + step + narrow, narrow)
        first = y_base + j * y_rows
        parts = [
            remote(
                basis_hbm.at[:, from_y, :, lanes_of(ct)], border.at[ct, pl.ds(first + core * size_x, size_x)],
                out_send.at[j], face_recv.at[j], peer(me_w, k), n,
            )
            for k in range(CORES) for ct in range(slices)
        ]
        came = arrival(border.at[:, pl.ds(first, y_rows)], out_send.at[j], face_recv.at[j])
        faces.append((
            parts, jnp.logical_and(me_n + step >= 0, me_n + step < narrow), came,
            [(came, jnp.logical_and(me_n - step >= 0, me_n - step < narrow))],
        ))
    toward = chip + 2 * core - 1
    x_to = lax.rem(toward + chips, chips)
    parts = [
        remote(
            basis_hbm.at[core * (size_x - 1), :, :, lanes_of(ct)], border.at[ct, pl.ds(core * x_base[0], x_rows)],
            out_send.at[2], face_recv.at[2 + core], CORES * x_to + k, me_n,
        )
        for k in range(CORES) for ct in range(slices)
    ]
    faces.append((
        parts, jnp.logical_and(toward >= 0, toward < chips),
        arrival(border.at[:, pl.ds(0, CORES * x_rows)], out_send.at[2], face_recv.at[2]),
        [
            (arrival(border.at[:, pl.ds(k * x_base[0], x_rows)], out_send.at[2], face_recv.at[2 + k]), there)
            for k, there in ((0, chip < chips - 1), (1, chip > 0))
        ],
    ))
    for parts, sends, gone, comes in faces:
        def go(parts=parts):
            for part in parts:
                part.start()
        pl.when(sends)(go)
    mate = [
        remote(
            basis_hbm.at[:, :, :, lanes_of(ct)], basis.at[ct, mine_x],
            out_send.at[3], mate_recv.at[0], peer(me_w, 1), me_n,
        )
        for ct in range(slices)
    ]
    for part in mate:
        part.start()
    mate_gone = arrival(basis.at[:, mine_x], out_send.at[3], mate_recv.at[0])
    mate_back = arrival(basis.at[:, theirs_x], out_send.at[3], mate_recv.at[0])
    mate_kappa = remote(kappa_hbm, kappa.at[core], out_send.at[4], mate_recv.at[1], peer(me_w, 1), me_n)
    mate_kappa.start()

    loaded.wait()
    started.wait()

    def arrange(first, blocks, keep):
        values = jnp.concatenate([block.reshape(-1, LANES) for block in blocks], axis=1)
        count = values.shape[0]
        if keep:
            rows_of[pl.ds(first, count), :] = values
        columns_of[:, pl.ds(first, count)] = values.T

    arrange(pl.multiple_of(core * half, half), [basis[ct, mine_x] for ct in range(slices)], True)

    speeds.wait()
    own_kappa.wait()
    for k in range(3):
        speed[k] = (0.25 * jnp.broadcast_to(velocity[k:k + 1, :], (LANES, samples))).T

    all_in_go_on()
    mate_back.wait_recv()
    mate_kappa.wait_recv()
    arrange(pl.multiple_of((1 - core) * half, half), [basis[ct, theirs_x] for ct in range(slices)], True)

    def rounded(rows, at):
        return dot(rows, columns_of[:, at], NN).astype(bf16).astype(f32)

    first_rows = jnp.concatenate([
        coefficients[peer(chip, e), peer(me_n, d)].astype(bf16) for d in range(narrow) for e in range(chips)
    ], axis=0)
    inner, outer = slice(0, cells), slice(cells, cells + border.shape[1] * size_z)
    field[:, inner] = rounded(first_rows, inner)

    cell = lax.broadcasted_iota(jnp.int32, (1, cells), 1)
    y_of, z_of = (cell % pitch) // size_z, cell % size_z
    pick = (y_of == lax.broadcasted_iota(jnp.int32, (size_y, cells), 0)).astype(bf16)
    line = lax.broadcasted_iota(jnp.int32, (depth * size_z, cells), 0)
    own_row = (line == (cell // pitch) * size_z + z_of).astype(f32)
    rest = kappa[...].reshape(depth * size_z, size_y)
    found = jnp.zeros((depth * size_z, cells), f32)
    for _ in range(3):
        part = rest.astype(bf16)
        rest = rest - part.astype(f32)
        found = found + dot(part, pick, NN)
    factor[...] = jnp.broadcast_to(jnp.sum(found * own_row, axis=0, keepdims=True), factor.shape)

    for parts, sends, gone, comes in faces:
        for came, there in comes:
            pl.when(there)(came.wait_recv)
    arrange(cells, [border[ct] for ct in range(slices)], False)
    field[:, outer] = rounded(first_rows, outer)

    lane = lax.broadcasted_iota(jnp.int32, (8, LANES), 1)
    lane_x, lane_y, lane_z = lane // pitch, (lane % pitch) // size_z, lane % size_z
    per_tile = LANES // pitch
    low_y, high_y = lane_y == 0, lane_y == size_y - 1
    first_of_tile, last_of_tile = lane < pitch, lane >= LANES - pitch
    from_border = lane_x * size_z + lane_z + jnp.where(high_y, y_rows * size_z, 0)
    z_sign = jnp.where(lane_z == 0, 1.0, -1.0)

    def stencil(first, speeds_of):
        def at(t):
            return field[first:first + 8, t * LANES:(t + 1) * LANES]

        def turn(value, by):
            return pltpu.roll(value, by % LANES, 1)

        v_x, v_y, v_z = speeds_of
        if size_z == 2:
            v_z = v_z * z_sign
        center = [at(t) for t in range(tiles + 1)]
        ahead = [turn(value, -pitch) for value in center]
        behind = [turn(value, pitch) for value in center]
        y_border = at(tiles + 1)
        out = []
        for t in range(tiles):
            mid = center[t]
            x_next = jnp.where(last_of_tile, ahead[t + 1], ahead[t])
            x_prev = jnp.where(first_of_tile, behind[t - 1], behind[t])
            outside = jnp.take_along_axis(y_border, from_border + t * per_tile * size_z, axis=1)
            y_next = jnp.where(high_y, outside, turn(mid, -size_z))
            y_prev = jnp.where(low_y, outside, turn(mid, size_z))
            x_sum, y_sum = x_next + x_prev, y_next + y_prev
            carried = v_x * (x_sum * (x_next - x_prev)) + v_y * (y_sum * (y_next - y_prev))
            if size_z == 2:
                z_sum = jnp.where(lane_z == 0, turn(mid, -1), turn(mid, 1))
                carried = carried + v_z * (z_sum * z_sum)
            else:
                z_next = jnp.where(lane_z < size_z - 1, turn(mid, -1), 0.0)
                z_prev = jnp.where(lane_z > 0, turn(mid, 1), 0.0)
                z_sum = z_next + z_prev
                carried = carried + v_z * (z_sum * (z_next - z_prev))
            spread = x_sum + y_sum + z_sum - 6.0 * mid
            out.append(factor[:, t * LANES:(t + 1) * LANES] * spread - carried)
        return jnp.concatenate(out, axis=1)

    def speeds_at(d, g):
        pieces = [[], [], []]
        for r in range(8 * g, 8 * g + 8, min(8, owned)):
            e, inner = r // owned, r % owned
            row = ((CORES * peer(chip, e) + core) * narrow + peer(me_n, d)) * owned + inner
            count = min(8, owned)
            if count % 8 == 0:
                row = pl.multiple_of(row, 8)
            for k in range(3):
                pieces[k].append(speed[k, pl.ds(row, count), :])
        return [jnp.concatenate(p, axis=0) if len(p) > 1 else p[0] for p in pieces]

    def slot(d, e):
        return d * chips + e - 1

    def scatter(group):
        forcing = jnp.concatenate(
            [stencil(d * unit + 8 * g, speeds_at(d, g)) for d in group for g in range(unit // 8)], axis=0
        ).astype(bf16)
        total = dot(forcing, rows_of[...], NN)
        copies = []
        for i, d in enumerate(group):
            for e in reversed(range(chips)):
                block = total[i * unit + e * owned:i * unit + (e + 1) * owned]
                if d + e == 0:
                    kept[...] = block
                    continue
                reduced[slot(d, e)] = block.astype(WIRE)
                copies.append(remote(
                    reduced.at[slot(d, e)], landed.at[slot(d, e)], r_send, r_recv,
                    CORES * peer(chip, e) + core, peer(me_n, d),
                ))
        return copies

    def each(there):
        for d in range(narrow):
            for e in range(chips):
                if d + e > 0:
                    there(d, e)

    def reduced_sent():
        arrival(reduced, r_send, r_recv).wait_send()

    def mine_sent():
        arrival(reduced, g_send, r_recv).wait_send()

    near_first = [tuple(range(narrow // 2))] + [(d,) for d in range(narrow // 2, narrow)]
    far_first = [tuple(range(narrow // 2, narrow))[::-1], tuple(range(narrow // 2))[::-1]]
    state = coefficients[chip, me_n]
    for step in range(ITERS):
        if step > 0:
            reduced_sent()
        for number, group in enumerate(near_first if step else far_first):
            if step > 0:
                blocks = []
                for d in group:
                    beyond = gathered.at[d] if d > 0 else gathered.at[0, pl.ds(1, chips - 1)]
                    arrival(beyond, g_send, g_recv.at[d]).wait_recv()
                for d in group:
                    for e in range(chips):
                        blocks.append(gathered[d, e] if d + e > 0 else mine[...])
                rows = jnp.concatenate(blocks, axis=0)
                at = slice(group[0] * unit, (group[-1] + 1) * unit)
                field[at, :] = rounded(rows, slice(None))
            copies = scatter(group)
            if step == 0 and number == 0:
                all_in()
            for copy in copies:
                copy.start()

        if step == 0:
            inverse.wait()
            high = propagator[...].astype(bf16)
            g_high[...] = high.T
            g_low[...] = (propagator[...] - high.astype(f32)).astype(bf16).T

        arrival(landed, r_send, r_recv).wait_recv()
        parts = [kept[...]]
        each(lambda d, e: parts.append(landed[slot(d, e)].astype(f32)))
        summed = sum(parts[1:], parts[0])

        update = state + step_size * (summed * scale)
        high = update.astype(bf16)
        low = (update - high.astype(f32)).astype(bf16)
        both = dot(jnp.concatenate([high, low], axis=0), g_high[...], NN)
        small = both[owned:] + dot(high, g_low[...], NN)
        state = update + (both[:owned] + small)

        if step + 1 < ITERS:
            if step > 0:
                mine_sent()
            mine[...] = state.astype(bf16)
            for d in reversed(range(narrow)):
                for e in reversed(range(chips)):
                    if d + e > 0:
                        remote(
                            mine, gathered.at[d, e], g_send, g_recv.at[d],
                            CORES * peer(chip, e) + core, peer(me_n, d),
                        ).start()

    out_ref[...] = state
    reduced_sent()
    mine_sent()
    for parts, sends, gone, comes in faces:
        pl.when(sends)(gone.wait_send)
    mate_gone.wait_send()
    mate_kappa.wait_send()


def body(basis, kappa, velocity, coefficients, propagator):
    size_x, size_y, size_z, modes = basis.shape
    samples = coefficients.shape[0]
    wide, narrow = lax.axis_size("wide"), lax.axis_size("narrow")
    chips = wide // CORES
    owned = samples // (wide * narrow)
    unit = chips * owned
    scale = 1.0 / math.sqrt(size_x * size_y * size_z * wide * narrow)
    pitch = size_y * size_z
    depth = CORES * size_x
    cells = depth * pitch
    assert LANES % pitch == 0 and cells % LANES == 0 and 2 * pitch <= LANES
    assert 2 * depth * size_z == LANES and unit % 8 == 0
    border = 2 * LANES // size_z
    dma = pltpu.SemaphoreType.DMA
    hbm = pl.BlockSpec(memory_space=pltpu.HBM)
    inputs = (
        basis, kappa.transpose(0, 2, 1), velocity,
        coefficients.reshape(wide, narrow, owned, modes), propagator,
    )
    return pl.pallas_call(
        functools.partial(kernel, chips, narrow, scale),
        out_shape=jax.ShapeDtypeStruct((owned, modes), f32),
        in_specs=[hbm] * len(inputs),
        out_specs=pl.BlockSpec(memory_space=pltpu.VMEM),
        scratch_shapes=[
            pltpu.VMEM((modes // LANES, depth, size_y, size_z, LANES), bf16),
            pltpu.VMEM((modes // LANES, border, size_z, LANES), bf16),
            pltpu.VMEM((CORES, size_x, size_z, size_y), f32),
            pltpu.VMEM((3, samples), f32),
            pltpu.VMEM((chips, narrow, owned, modes), f32),
            pltpu.VMEM((modes, modes), f32),
            pltpu.VMEM((cells, modes), bf16),
            pltpu.VMEM((modes, cells + border * size_z), bf16),
            pltpu.VMEM((narrow * unit, cells + border * size_z), f32),
            pltpu.VMEM((8, cells), f32),
            pltpu.VMEM((3, samples, LANES), f32),
            pltpu.VMEM((modes, modes), bf16),
            pltpu.VMEM((modes, modes), bf16),
            pltpu.VMEM((narrow * chips - 1, owned, modes), WIRE),
            pltpu.VMEM((narrow * chips - 1, owned, modes), WIRE),
            pltpu.VMEM((owned, modes), f32),
            pltpu.VMEM((owned, modes), bf16),
            pltpu.VMEM((narrow, chips, owned, modes), bf16),
            dma((5,)), dma((2,)), dma((4,)), dma((5,)), dma, dma, dma, dma((narrow,)),
            pltpu.SemaphoreType.REGULAR((4 if chips > 2 else 2,)),
        ],
        compiler_params=pltpu.CompilerParams(
            collective_id=0, has_side_effects=True, vmem_limit_bytes=48 * 1024 * 1024
        ),
    )(*(pltpu.with_memory_space_constraint(value, pltpu.HBM) for value in inputs))


def solution(mesh):
    placed = (
        P(("groups", "wide"), "narrow", None, None),
        P(("groups", "wide"), "narrow", None),
        P(None, "groups"),
        P("groups", None),
        P("groups", None),
    )
    return jax.shard_map(
        body,
        mesh=mesh,
        in_specs=placed,
        out_specs=P(("groups", "wide", "narrow"), None),
        check_vma=False,
    )
```

time: 30.1 us -> 25.5 us (0.85)
  Pallas kernels: 29.3 us -> 24.7 us
    pallas_call x1, Pallas kernels: 29.3 us -> 24.7 us  [body(): pl.pallas_call(functools.partial(kernel, chips, narrow, scale), out_shape...]
where the time goes in v2:
time: 25.5 us; the launch traced here: 25.4 us
  Pallas kernels  24.7 us (97%)
  local copies, waits for them, and re-layouts  0.62 us (2%)
    pallas_call x1, Pallas kernels, body(): pl.pallas_call(functools.partial(kernel, chips, narrow, scale), out_shape...  24.7 us
    unnamed x1, local copies, waits for them, and re-layouts  0.62 us

profile of v2, /device:TPU:0, one launch (start us, length us, event | category | flops | bytes accessed | tf_op | source)
XLA Modules:
  0.0 25.4 jit_solution(10175384089016458851)
XLA Ops:
  0.0 24.7 %shard_map.55 = f32[16,512]{1,0:T(8,128)S(1)} custom-call(bf16[16,16,2,512]{3,2,1,0:T(2,128)(2,1)} %basis_hbm.1, f32[16,2,16]{2,1,0:T(2,128)} %bitcast.3, f32[3,256]{1,0:T(4,128)} %velocity_hbm.1, f32[4,4,16,512]{3,2,1,0:T(8,128)} %bitcast.2, f32[512,512]{1,0:T(8,128)} %propagator_hbm.1), custom_call_target="tpu_custom_call" | custom-call | tf_op jit(solution)/shard_map/pallas_call | solution.py:438
  24.7 0.6 %copy.7 = f32[16,512]{1,0:T(8,128)} copy(f32[16,512]{1,0:T(8,128)S(1)} %shard_map.55) | data formatting | bytes 65536

commit v3 on v2

--- a/solution.py
+++ b/solution.py
@@ -37,10 +37,10 @@
     chips, narrow, scale,
     basis_hbm, kappa_hbm, velocity_hbm, coefficients_hbm, propagator_hbm, out_ref,
     basis, border, kappa, velocity, coefficients, propagator,
-    rows_of, columns_of, field, factor, speed, g_high, g_low,
+    edge_out, edge_in, edge_of, rows_of, columns_of, field, factor, speed, g_high, g_low,
     reduced, landed, kept, mine, gathered,
     load_sem, mate_recv, face_recv, out_send,
-    r_send, r_recv, g_send, g_recv, word,
+    r_send, r_recv, g_send, g_recv, edge_send, edge_recv, word,
 ):
     size_x, size_y, size_z, modes = basis_hbm.shape
     slices, depth = basis.shape[:2]
@@ -56,6 +56,7 @@
     wide = chips * CORES
     me_w, me_n = lax.axis_index("wide"), lax.axis_index("narrow")
     chip, core = me_w // CORES, me_w % CORES
+    far_x, far_n = chips // 2, narrow // 2
 
     def lanes_of(ct):
         return pl.ds(ct * LANES, LANES)
@@ -93,22 +94,18 @@
     loaded = pltpu.make_async_copy(basis.at[:, mine_x], basis.at[:, mine_x], load_sem.at[0])
     for load in loads:
         load.start()
-    starts = [
-        pltpu.make_async_copy(coefficients_hbm.at[CORES * x + core], coefficients.at[x], load_sem.at[3])
-        for x in range(chips)
-    ]
-    started = pltpu.make_async_copy(coefficients, coefficients, load_sem.at[3])
-    for start in starts:
-        start.start()
+    started = pltpu.make_async_copy(coefficients_hbm, coefficients, load_sem.at[3])
+    started.start()
     own_kappa = pltpu.make_async_copy(kappa_hbm, kappa.at[core], load_sem.at[1])
     own_kappa.start()
     speeds = pltpu.make_async_copy(velocity_hbm, velocity, load_sem.at[4])
     speeds.start()
     inverse = pltpu.make_async_copy(propagator_hbm, propagator, load_sem.at[2])
-    inverse.start()
 
     def clear(first, count):
         border[:, pl.ds(first, count)] = jnp.zeros((slices, count) + border.shape[2:], bf16)
+        at = slice(first * size_z, (first + count) * size_z)
+        edge_in[at, :] = jnp.zeros((count * size_z, edge_in.shape[1]), bf16)
 
     pl.when(chip == 0)(lambda: clear(x_base[0], x_rows))
     pl.when(chip == chips - 1)(lambda: clear(x_base[1], x_rows))
@@ -160,7 +157,23 @@
     def arrival(ref, send, recv):
         return remote(ref, ref, send, recv, me_w, me_n)
 
-    faces = []
+    faces, edges = [], []
+    line_x, line_y = size_y * size_z, size_x * size_z
+
+    def edge(face, first, count, number, came, w, n):
+        parts = [
+            remote(
+                edge_out.at[k, pl.ds(face[0], face[1])], edge_in.at[pl.ds(first, count)],
+                edge_send.at[number], edge_recv.at[came], w(k), n,
+            )
+            for k in range(CORES)
+        ]
+        gone = arrival(edge_in.at[pl.ds(0, CORES * count)], edge_send.at[number], edge_recv.at[came])
+        return parts, gone
+
+    def whole_edge(first, count, number):
+        return arrival(edge_in.at[pl.ds(first * size_z, count * size_z)], edge_send.at[0], edge_recv.at[number])
+
     for j, (from_y, step) in enumerate(((size_y - 1, 1), (0, -1))):
         n = lax.rem(me_n + step + narrow, narrow)
         first = y_base + j * y_rows
@@ -172,10 +185,12 @@
             for k in range(CORES) for ct in range(slices)
         ]
         came = arrival(border.at[:, pl.ds(first, y_rows)], out_send.at[j], face_recv.at[j])
-        faces.append((
-            parts, jnp.logical_and(me_n + step >= 0, me_n + step < narrow), came,
-            [(came, jnp.logical_and(me_n - step >= 0, me_n - step < narrow))],
-        ))
+        goes = jnp.logical_and(me_n + step >= 0, me_n + step < narrow)
+        there = jnp.logical_and(me_n - step >= 0, me_n - step < narrow)
+        faces.append((parts, goes, came, [(came, there)]))
+        at = pl.multiple_of(first * size_z + core * line_y, line_y)
+        parts, gone = edge((j * line_y, line_y), at, line_y, j, j, lambda k: CORES * chip + k, n)
+        edges.append((parts, goes, gone, [(whole_edge(first, y_rows, j), there)]))
     toward = chip + 2 * core - 1
     x_to = lax.rem(toward + chips, chips)
     parts = [
@@ -185,19 +200,33 @@
         )
         for k in range(CORES) for ct in range(slices)
     ]
+    goes = jnp.logical_and(toward >= 0, toward < chips)
     faces.append((
-        parts, jnp.logical_and(toward >= 0, toward < chips),
+        parts, goes,
         arrival(border.at[:, pl.ds(0, CORES * x_rows)], out_send.at[2], face_recv.at[2]),
         [
             (arrival(border.at[:, pl.ds(k * x_base[0], x_rows)], out_send.at[2], face_recv.at[2 + k]), there)
             for k, there in ((0, chip < chips - 1), (1, chip > 0))
         ],
     ))
-    for parts, sends, gone, comes in faces:
-        def go(parts=parts):
-            for part in parts:
-                part.start()
-        pl.when(sends)(go)
+    at = pl.multiple_of(core * (x_base[0] * size_z), line_x)
+    parts, gone = edge((2 * line_y, line_x), at, line_x, 2, 2 + core, lambda k: CORES * x_to + k, me_n)
+    edges.append((parts, goes, gone, [
+        (whole_edge(k * x_base[0], x_rows, 2 + k), there) for k, there in ((0, chip < chips - 1), (1, chip > 0))
+    ]))
+
+    def send_all(copies):
+        for parts, sends, gone, comes in copies:
+            def go(parts=parts):
+                for part in parts:
+                    part.start()
+            pl.when(sends)(go)
+
+    def take_all(copies):
+        for parts, sends, gone, comes in copies:
+            for came, there in comes:
+                pl.when(there)(came.wait_recv)
+
     mate = [
         remote(
             basis_hbm.at[:, :, :, lanes_of(ct)], basis.at[ct, mine_x],
@@ -214,15 +243,32 @@
 
     loaded.wait()
     started.wait()
-
-    def arrange(first, blocks, keep):
-        values = jnp.concatenate([block.reshape(-1, LANES) for block in blocks], axis=1)
+    inverse.start()
+
+    def in_tiles(of):
+        return jnp.concatenate([of(ct).reshape(-1, LANES) for ct in range(slices)], axis=1)
+
+    own_edge = jnp.concatenate([
+        in_tiles(lambda ct: basis[ct, mine_x, size_y - 1]), in_tiles(lambda ct: basis[ct, mine_x, 0]),
+        in_tiles(lambda ct: basis[ct, core * (depth - 1)]),
+    ], axis=0)
+    those = jnp.concatenate([
+        coefficients[CORES * x + k].reshape(narrow * owned, modes).astype(bf16)
+        for k in range(CORES) for x in range(chips)
+    ], axis=0)
+    on_edge = dot(own_edge, those, NT).astype(bf16)
+    for k in range(CORES):
+        edge_out[k] = on_edge[:, k * narrow * unit:(k + 1) * narrow * unit]
+    send_all(edges)
+    send_all(faces)
+
+    def arrange(first, values, keep):
         count = values.shape[0]
         if keep:
             rows_of[pl.ds(first, count), :] = values
         columns_of[:, pl.ds(first, count)] = values.T
 
-    arrange(pl.multiple_of(core * half, half), [basis[ct, mine_x] for ct in range(slices)], True)
+    arrange(pl.multiple_of(core * half, half), in_tiles(lambda ct: basis[ct, mine_x]), True)
 
     speeds.wait()
     own_kappa.wait()
@@ -232,15 +278,16 @@
     all_in_go_on()
     mate_back.wait_recv()
     mate_kappa.wait_recv()
-    arrange(pl.multiple_of((1 - core) * half, half), [basis[ct, theirs_x] for ct in range(slices)], True)
+    arrange(pl.multiple_of((1 - core) * half, half), in_tiles(lambda ct: basis[ct, theirs_x]), True)
 
     def rounded(rows, at):
         return dot(rows, columns_of[:, at], NN).astype(bf16).astype(f32)
 
     first_rows = jnp.concatenate([
-        coefficients[peer(chip, e), peer(me_n, d)].astype(bf16) for d in range(narrow) for e in range(chips)
+        coefficients[CORES * peer(chip, e ^ far_x) + core, peer(me_n, d ^ far_n)].astype(bf16)
+        for d in range(narrow) for e in range(chips)
     ], axis=0)
-    inner, outer = slice(0, cells), slice(cells, cells + border.shape[1] * size_z)
+    inner = slice(0, cells)
     field[:, inner] = rounded(first_rows, inner)
 
     cell = lax.broadcasted_iota(jnp.int32, (1, cells), 1)
@@ -256,11 +303,9 @@
         found = found + dot(part, pick, NN)
     factor[...] = jnp.broadcast_to(jnp.sum(found * own_row, axis=0, keepdims=True), factor.shape)
 
-    for parts, sends, gone, comes in faces:
-        for came, there in comes:
-            pl.when(there)(came.wait_recv)
-    arrange(cells, [border[ct] for ct in range(slices)], False)
-    field[:, outer] = rounded(first_rows, outer)
+    take_all(edges)
+    for k in range(edge_of.shape[0]):
+        edge_of[k] = edge_in[k * LANES:(k + 1) * LANES, :].T.astype(f32)
 
     lane = lax.broadcasted_iota(jnp.int32, (8, LANES), 1)
     lane_x, lane_y, lane_z = lane // pitch, (lane % pitch) // size_z, lane % size_z
@@ -270,8 +315,10 @@
     from_border = lane_x * size_z + lane_z + jnp.where(high_y, y_rows * size_z, 0)
     z_sign = jnp.where(lane_z == 0, 1.0, -1.0)
 
-    def stencil(first, speeds_of):
+    def stencil(first, speeds_of, edge_rows):
         def at(t):
+            if t >= tiles and edge_rows:
+                return joined([edge_of[t - tiles, pl.ds(row, count), :] for row in edge_rows])
             return field[first:first + 8, t * LANES:(t + 1) * LANES]
 
         def turn(value, by):
@@ -306,38 +353,46 @@
             out.append(factor[:, t * LANES:(t + 1) * LANES] * spread - carried)
         return jnp.concatenate(out, axis=1)
 
-    def speeds_at(d, g):
-        pieces = [[], [], []]
-        for r in range(8 * g, 8 * g + 8, min(8, owned)):
-            e, inner = r // owned, r % owned
-            row = ((CORES * peer(chip, e) + core) * narrow + peer(me_n, d)) * owned + inner
-            count = min(8, owned)
-            if count % 8 == 0:
-                row = pl.multiple_of(row, 8)
-            for k in range(3):
-                pieces[k].append(speed[k, pl.ds(row, count), :])
-        return [jnp.concatenate(p, axis=0) if len(p) > 1 else p[0] for p in pieces]
+    count = min(8, owned)
+
+    def joined(pieces):
+        return jnp.concatenate(pieces, axis=0) if len(pieces) > 1 else pieces[0]
+
+    def places(first):
+        for row in range(first, first + 8, count):
+            d, e, inner = row // unit, row % unit // owned, row % owned
+            x, n = peer(chip, e ^ far_x), peer(me_n, d ^ far_n)
+            pair = (x * narrow + n) * owned + inner, ((CORES * x + core) * narrow + n) * owned + inner
+            yield tuple(pl.multiple_of(at, 8) for at in pair) if count == 8 else pair
+
+    def speeds_at(first):
+        rows = [at for _, at in places(first)]
+        return [joined([speed[k, pl.ds(at, count), :] for at in rows]) for k in range(3)]
 
     def slot(d, e):
         return d * chips + e - 1
 
-    def scatter(group):
-        forcing = jnp.concatenate(
-            [stencil(d * unit + 8 * g, speeds_at(d, g)) for d in group for g in range(unit // 8)], axis=0
-        ).astype(bf16)
-        total = dot(forcing, rows_of[...], NN)
+    def scatter(group, step, residue):
+        made = []
+        for first in rows_in(group):
+            edge_rows = [at for at, _ in places(first)] if step == 0 else []
+            made.append(stencil(first, speeds_at(first), edge_rows))
+        total = dot(jnp.concatenate(made, axis=0).astype(bf16), rows_of[...], NN)
         copies = []
-        for i, d in enumerate(group):
-            for e in reversed(range(chips)):
-                block = total[i * unit + e * owned:i * unit + (e + 1) * owned]
-                if d + e == 0:
-                    kept[...] = block
-                    continue
-                reduced[slot(d, e)] = block.astype(WIRE)
-                copies.append(remote(
-                    reduced.at[slot(d, e)], landed.at[slot(d, e)], r_send, r_recv,
-                    CORES * peer(chip, e) + core, peer(me_n, d),
-                ))
+        for i, (d, e) in enumerate(group):
+            block = total[i * owned:(i + 1) * owned]
+            if step == ITERS - 1 and d + e == 0 and far_n + far_x > 0:
+                block = block + residue * (1.0 / (step_size * scale))
+            to_n, to_x = (d ^ far_n, e ^ far_x) if step == ITERS - 1 else (d, e)
+            if to_n + to_x == 0:
+                kept[...] = block
+                continue
+            at = slot(to_n, to_x)
+            reduced[at] = block.astype(WIRE)
+            copies.append(remote(
+                reduced.at[at], landed.at[step, at], r_send, r_recv.at[step],
+                CORES * peer(chip, to_x) + core, peer(me_n, to_n),
+            ))
         return copies
 
     def each(there):
@@ -347,46 +402,65 @@
                     there(d, e)
 
     def reduced_sent():
-        arrival(reduced, r_send, r_recv).wait_send()
+        arrival(reduced, r_send, r_recv.at[0]).wait_send()
 
     def mine_sent():
-        arrival(reduced, g_send, r_recv).wait_send()
-
-    near_first = [tuple(range(narrow // 2))] + [(d,) for d in range(narrow // 2, narrow)]
-    far_first = [tuple(range(narrow // 2, narrow))[::-1], tuple(range(narrow // 2))[::-1]]
-    state = coefficients[chip, me_n]
+        arrival(reduced, g_send, r_recv.at[0]).wait_send()
+
+    blocks_of = [[(d, e) for e in reversed(range(chips))] for d in range(narrow)]
+    nearer, farther = range(narrow // 2), range(narrow // 2, narrow)
+    if owned % 8 == 0:
+        far_first = [blocks_of[d] for d in reversed(farther)]
+        far_first.append(sum((blocks_of[d] for d in reversed(nearer)), []))
+        near_first = [[(0, 0)], [(0, e) for e in range(1, chips)]]
+        near_first += [blocks_of[d][::-1] for d in nearer if d > 0]
+        near_first.append(sum((blocks_of[d][::-1] for d in farther), []))
+        near_first = [group for group in near_first if group]
+    else:
+        far_first = [sum((blocks_of[d][::-1] for d in part), []) for part in (farther, nearer)]
+        near_first = far_first[::-1]
+
+    def rows_in(group):
+        if owned % 8 == 0:
+            return [(d * chips + e) * owned + inner for d, e in group for inner in range(0, owned, 8)]
+        return range(group[0][0] * unit, (group[-1][0] + 1) * unit, 8)
+
+    state = coefficients[CORES * peer(chip, far_x) + core, peer(me_n, far_n)]
+    residue = None
     for step in range(ITERS):
         if step > 0:
             reduced_sent()
         for number, group in enumerate(near_first if step else far_first):
             if step > 0:
-                blocks = []
-                for d in group:
+                for d in sorted({d for d, e in group if d > 0 or e > 0}):
                     beyond = gathered.at[d] if d > 0 else gathered.at[0, pl.ds(1, chips - 1)]
                     arrival(beyond, g_send, g_recv.at[d]).wait_recv()
-                for d in group:
-                    for e in range(chips):
-                        blocks.append(gathered[d, e] if d + e > 0 else mine[...])
-                rows = jnp.concatenate(blocks, axis=0)
-                at = slice(group[0] * unit, (group[-1] + 1) * unit)
-                field[at, :] = rounded(rows, slice(None))
-            copies = scatter(group)
+                rows = jnp.concatenate([gathered[d, e] if d + e > 0 else mine[...] for d, e in group], axis=0)
+                made = rounded(rows, slice(None))
+                for i, (d, e) in enumerate(group):
+                    at = (d * chips + e) * owned
+                    field[at:at + owned, :] = made[i * owned:(i + 1) * owned]
+            copies = scatter(group, step, residue)
             if step == 0 and number == 0:
                 all_in()
             for copy in copies:
                 copy.start()
 
         if step == 0:
+            take_all(faces)
+            arrange(cells, in_tiles(lambda ct: border[ct]), False)
             inverse.wait()
             high = propagator[...].astype(bf16)
             g_high[...] = high.T
             g_low[...] = (propagator[...] - high.astype(f32)).astype(bf16).T
 
-        arrival(landed, r_send, r_recv).wait_recv()
+        arrival(landed.at[step], r_send, r_recv.at[step]).wait_recv()
         parts = [kept[...]]
-        each(lambda d, e: parts.append(landed[slot(d, e)].astype(f32)))
+        each(lambda d, e: parts.append(landed[step, slot(d, e)].astype(f32)))
         summed = sum(parts[1:], parts[0])
 
+        if step == ITERS - 1 and far_n + far_x > 0:
+            state = gathered[far_n, far_x].astype(f32)
         update = state + step_size * (summed * scale)
         high = update.astype(bf16)
         low = (update - high.astype(f32)).astype(bf16)
@@ -398,7 +472,8 @@
             if step > 0:
                 mine_sent()
             mine[...] = state.astype(bf16)
-            for d in reversed(range(narrow)):
+            residue = state - state.astype(bf16).astype(f32)
+            for d in [*reversed(nearer), *reversed(farther)]:
                 for e in reversed(range(chips)):
                     if d + e > 0:
                         remote(
@@ -409,7 +484,7 @@
     out_ref[...] = state
     reduced_sent()
     mine_sent()
-    for parts, sends, gone, comes in faces:
+    for parts, sends, gone, comes in faces + edges:
         pl.when(sends)(gone.wait_send)
     mate_gone.wait_send()
     mate_kappa.wait_send()
@@ -445,8 +520,11 @@
             pltpu.VMEM((modes // LANES, border, size_z, LANES), bf16),
             pltpu.VMEM((CORES, size_x, size_z, size_y), f32),
             pltpu.VMEM((3, samples), f32),
-            pltpu.VMEM((chips, narrow, owned, modes), f32),
+            pltpu.VMEM((wide, narrow, owned, modes), f32),
             pltpu.VMEM((modes, modes), f32),
+            pltpu.VMEM((CORES, (2 * size_x + size_y) * size_z, narrow * unit), bf16),
+            pltpu.VMEM((border * size_z, narrow * unit), bf16),
+            pltpu.VMEM((border * size_z // LANES, narrow * unit, LANES), f32),
             pltpu.VMEM((cells, modes), bf16),
             pltpu.VMEM((modes, cells + border * size_z), bf16),
             pltpu.VMEM((narrow * unit, cells + border * size_z), f32),
@@ -455,11 +533,11 @@
             pltpu.VMEM((modes, modes), bf16),
             pltpu.VMEM((modes, modes), bf16),
             pltpu.VMEM((narrow * chips - 1, owned, modes), WIRE),
-            pltpu.VMEM((narrow * chips - 1, owned, modes), WIRE),
+            pltpu.VMEM((ITERS, narrow * chips - 1, owned, modes), WIRE),
             pltpu.VMEM((owned, modes), f32),
             pltpu.VMEM((owned, modes), bf16),
             pltpu.VMEM((narrow, chips, owned, modes), bf16),
-            dma((5,)), dma((2,)), dma((4,)), dma((5,)), dma, dma, dma, dma((narrow,)),
+            dma((5,)), dma((2,)), dma((4,)), dma((5,)), dma, dma((ITERS,)), dma, dma((narrow,)), dma((3,)), dma((4,)),
             pltpu.SemaphoreType.REGULAR((4 if chips > 2 else 2,)),
         ],
         compiler_params=pltpu.CompilerParams(

time: 25.5 us -> 23.9 us (0.937)
  Pallas kernels: 24.7 us -> 23.1 us
    pallas_call x1, Pallas kernels: 24.7 us -> 23.1 us  [body(): pl.pallas_call(functools.partial(kernel, chips, narrow, scale), out_shape...]
where the time goes in v3:
time: 23.9 us; the launch traced here: 23.8 us
  Pallas kernels  23.1 us (97%)
  local copies, waits for them, and re-layouts  0.62 us (3%)
    pallas_call x1, Pallas kernels, body(): pl.pallas_call(functools.partial(kernel, chips, narrow, scale), out_shape...  23.1 us
    unnamed x1, local copies, waits for them, and re-layouts  0.62 us

profile of v3, /device:TPU:0, one launch (start us, length us, event | category | flops | bytes accessed | tf_op | source)
XLA Modules:
  0.0 23.8 jit_solution(17706525980241188111)
XLA Ops:
  0.0 23.1 %shard_map.55 = f32[16,512]{1,0:T(8,128)S(1)} custom-call(bf16[16,16,2,512]{3,2,1,0:T(2,128)(2,1)} %basis_hbm.1, f32[16,2,16]{2,1,0:T(2,128)} %bitcast.3, f32[3,256]{1,0:T(4,128)} %velocity_hbm.1, f32[4,4,16,512]{3,2,1,0:T(8,128)} %bitcast.2, f32[512,512]{1,0:T(8,128)} %propagator_hbm.1), custom_call_target="tpu_custom_call" | custom-call | tf_op jit(solution)/shard_map/pallas_call | solution.py:513
  23.2 0.6 %copy.7 = f32[16,512]{1,0:T(8,128)} copy(f32[16,512]{1,0:T(8,128)S(1)} %shard_map.55) | data formatting | bytes 65536

commit v4 on v3

--- a/solution.py
+++ b/solution.py
@@ -37,11 +37,13 @@
     chips, narrow, scale,
     basis_hbm, kappa_hbm, velocity_hbm, coefficients_hbm, propagator_hbm, out_ref,
     basis, border, kappa, velocity, coefficients, propagator,
-    edge_out, edge_in, edge_of, rows_of, columns_of, field, factor, speed, g_high, g_low,
+    own_rows, edge_out, edge_in, edge_of, rows_of, columns_of, field, factor, speed, g_high, g_low,
     reduced, landed, kept, mine, gathered,
     load_sem, mate_recv, face_recv, out_send,
-    r_send, r_recv, g_send, g_recv, edge_send, edge_recv, word,
+    first_recv, edge_send, edge_recv, word,
 ):
+    r_send, g_send, g_recv = edge_send.at[0], edge_send.at[1], edge_recv
+    r_recv = [first_recv] + [mate_recv.at[k] for k in range(ITERS - 1)]
     size_x, size_y, size_z, modes = basis_hbm.shape
     slices, depth = basis.shape[:2]
     owned = coefficients.shape[2]
@@ -61,32 +63,17 @@
     def lanes_of(ct):
         return pl.ds(ct * LANES, LANES)
 
-    barrier = pltpu.get_barrier_semaphore()
-
-    def greet(w, n):
-        pl.semaphore_signal(
-            barrier, inc=1, device_id={"wide": w, "narrow": n}, device_id_type=pl.DeviceIdType.MESH
-        )
-
-    greet(peer(me_w, 1), me_n)
-    greetings = 1
-    for step in (-1, 1):
-        n, x = me_n + step, chip + step
-        n_there = jnp.logical_and(n >= 0, n < narrow)
-        x_there = jnp.logical_and(x >= 0, x < chips)
-
-        def along_narrow(n=n):
-            for k in range(CORES):
-                greet(peer(me_w, k), n)
-
-        def along_wide(x=x):
-            for k in range(CORES):
-                greet(CORES * x + k, me_n)
-
-        pl.when(n_there)(along_narrow)
-        pl.when(x_there)(along_wide)
-        greetings = greetings + CORES * (jnp.where(n_there, 1, 0) + jnp.where(x_there, 1, 0))
     mine_x, theirs_x = pl.ds(core * size_x, size_x), pl.ds((1 - core) * size_x, size_x)
+    started = pltpu.make_async_copy(coefficients_hbm, coefficients, load_sem.at[3])
+    started.start()
+    outer_rows = pltpu.make_async_copy(own_rows, own_rows, load_sem.at[2])
+    for ct in range(slices):
+        for first, count, face in (
+            (0, size_x, basis_hbm.at[:, size_y - 1, :, lanes_of(ct)]),
+            (size_x, size_x, basis_hbm.at[:, 0, :, lanes_of(ct)]),
+            (2 * size_x, size_y, basis_hbm.at[core * (size_x - 1), :, :, lanes_of(ct)]),
+        ):
+            pltpu.make_async_copy(face, own_rows.at[ct, pl.ds(first, count)], load_sem.at[2]).start()
     loads = [
         pltpu.make_async_copy(basis_hbm.at[:, :, :, lanes_of(ct)], basis.at[ct, mine_x], load_sem.at[0])
         for ct in range(slices)
@@ -94,13 +81,38 @@
     loaded = pltpu.make_async_copy(basis.at[:, mine_x], basis.at[:, mine_x], load_sem.at[0])
     for load in loads:
         load.start()
-    started = pltpu.make_async_copy(coefficients_hbm, coefficients, load_sem.at[3])
-    started.start()
     own_kappa = pltpu.make_async_copy(kappa_hbm, kappa.at[core], load_sem.at[1])
     own_kappa.start()
     speeds = pltpu.make_async_copy(velocity_hbm, velocity, load_sem.at[4])
     speeds.start()
-    inverse = pltpu.make_async_copy(propagator_hbm, propagator, load_sem.at[2])
+    inverse = pltpu.make_async_copy(propagator_hbm, propagator, load_sem.at[3])
+
+
+    barrier = pltpu.get_barrier_semaphore()
+
+    def greet(w, n):
+        pl.semaphore_signal(
+            barrier, inc=1, device_id={"wide": w, "narrow": n}, device_id_type=pl.DeviceIdType.MESH
+        )
+
+    greet(peer(me_w, 1), me_n)
+    greetings = 1
+    for step in (-1, 1):
+        n, x = me_n + step, chip + step
+        n_there = jnp.logical_and(n >= 0, n < narrow)
+        x_there = jnp.logical_and(x >= 0, x < chips)
+
+        def along_narrow(n=n):
+            for k in range(CORES):
+                greet(peer(me_w, k), n)
+
+        def along_wide(x=x):
+            for k in range(CORES):
+                greet(CORES * x + k, me_n)
+
+        pl.when(n_there)(along_narrow)
+        pl.when(x_there)(along_wide)
+        greetings = greetings + CORES * (jnp.where(n_there, 1, 0) + jnp.where(x_there, 1, 0))
 
     def clear(first, count):
         border[:, pl.ds(first, count)] = jnp.zeros((slices, count) + border.shape[2:], bf16)
@@ -124,26 +136,32 @@
             pl.when(at == 0)(lambda: tell(forth, 1))
             pl.when(at == count - 1)(lambda: tell(back, -1))
 
+        def pass_on(sem, step):
+            pl.semaphore_wait(sem, 1)
+            tell(sem, step)
+
+        def from_ends():
+            if count > 2:
+                pl.when(at == 1)(lambda: pass_on(forth, 1))
+                pl.when(at == count - 2)(lambda: pass_on(back, -1))
+
         def go_on():
-            @pl.when(jnp.logical_and(at > 0, at < count - 1))
-            def _():
-                pl.semaphore_wait(forth, 1)
-                tell(forth, 1)
-                pl.semaphore_wait(back, 1)
-                tell(back, -1)
+            if count > 3:
+                pl.when(jnp.logical_and(at > 1, at < count - 1))(lambda: pass_on(forth, 1))
+                pl.when(jnp.logical_and(at > 0, at < count - 2))(lambda: pass_on(back, -1))
 
         def end():
             pl.when(at == count - 1)(lambda: pl.semaphore_wait(forth, 1))
             pl.when(at == 0)(lambda: pl.semaphore_wait(back, 1))
 
-        return begin, go_on, end
+        return begin, from_ends, go_on, end
 
     if chips > 2:
         for phase in lines(
             chips, chip, lambda x: {"wide": CORES * x + core, "narrow": me_n}, word.at[2], word.at[3]
         ):
             phase()
-    all_in_begin, all_in_go_on, all_in = lines(
+    all_in_begin, all_in_from_ends, all_in_go_on, all_in = lines(
         narrow, me_n, lambda n: {"wide": me_w, "narrow": n}, word.at[0], word.at[1]
     )
     all_in_begin()
@@ -234,24 +252,17 @@
         )
         for ct in range(slices)
     ]
-    for part in mate:
-        part.start()
     mate_gone = arrival(basis.at[:, mine_x], out_send.at[3], mate_recv.at[0])
     mate_back = arrival(basis.at[:, theirs_x], out_send.at[3], mate_recv.at[0])
     mate_kappa = remote(kappa_hbm, kappa.at[core], out_send.at[4], mate_recv.at[1], peer(me_w, 1), me_n)
-    mate_kappa.start()
-
-    loaded.wait()
+
     started.wait()
-    inverse.start()
+    outer_rows.wait()
 
     def in_tiles(of):
         return jnp.concatenate([of(ct).reshape(-1, LANES) for ct in range(slices)], axis=1)
 
-    own_edge = jnp.concatenate([
-        in_tiles(lambda ct: basis[ct, mine_x, size_y - 1]), in_tiles(lambda ct: basis[ct, mine_x, 0]),
-        in_tiles(lambda ct: basis[ct, core * (depth - 1)]),
-    ], axis=0)
+    own_edge = in_tiles(lambda ct: own_rows[ct])
     those = jnp.concatenate([
         coefficients[CORES * x + k].reshape(narrow * owned, modes).astype(bf16)
         for k in range(CORES) for x in range(chips)
@@ -260,6 +271,9 @@
     for k in range(CORES):
         edge_out[k] = on_edge[:, k * narrow * unit:(k + 1) * narrow * unit]
     send_all(edges)
+    for part in mate:
+        part.start()
+    mate_kappa.start()
     send_all(faces)
 
     def arrange(first, values, keep):
@@ -268,6 +282,8 @@
             rows_of[pl.ds(first, count), :] = values
         columns_of[:, pl.ds(first, count)] = values.T
 
+    loaded.wait()
+    inverse.start()
     arrange(pl.multiple_of(core * half, half), in_tiles(lambda ct: basis[ct, mine_x]), True)
 
     speeds.wait()
@@ -275,7 +291,7 @@
     for k in range(3):
         speed[k] = (0.25 * jnp.broadcast_to(velocity[k:k + 1, :], (LANES, samples))).T
 
-    all_in_go_on()
+    all_in_from_ends()
     mate_back.wait_recv()
     mate_kappa.wait_recv()
     arrange(pl.multiple_of((1 - core) * half, half), in_tiles(lambda ct: basis[ct, theirs_x]), True)
@@ -303,6 +319,7 @@
         found = found + dot(part, pick, NN)
     factor[...] = jnp.broadcast_to(jnp.sum(found * own_row, axis=0, keepdims=True), factor.shape)
 
+    all_in_go_on()
     take_all(edges)
     for k in range(edge_of.shape[0]):
         edge_of[k] = edge_in[k * LANES:(k + 1) * LANES, :].T.astype(f32)
@@ -390,7 +407,7 @@
             at = slot(to_n, to_x)
             reduced[at] = block.astype(WIRE)
             copies.append(remote(
-                reduced.at[at], landed.at[step, at], r_send, r_recv.at[step],
+                reduced.at[at], landed.at[step, at], r_send, r_recv[step],
                 CORES * peer(chip, to_x) + core, peer(me_n, to_n),
             ))
         return copies
@@ -402,10 +419,10 @@
                     there(d, e)
 
     def reduced_sent():
-        arrival(reduced, r_send, r_recv.at[0]).wait_send()
+        arrival(reduced, r_send, r_recv[0]).wait_send()
 
     def mine_sent():
-        arrival(reduced, g_send, r_recv.at[0]).wait_send()
+        arrival(reduced, g_send, r_recv[0]).wait_send()
 
     blocks_of = [[(d, e) for e in reversed(range(chips))] for d in range(narrow)]
     nearer, farther = range(narrow // 2), range(narrow // 2, narrow)
@@ -440,11 +457,17 @@
                 for i, (d, e) in enumerate(group):
                     at = (d * chips + e) * owned
                     field[at:at + owned, :] = made[i * owned:(i + 1) * owned]
-            copies = scatter(group, step, residue)
-            if step == 0 and number == 0:
-                all_in()
-            for copy in copies:
-                copy.start()
+            parts = [group]
+            if step > 0 and group is near_first[-1] and owned % 8 == 0 and len(group) > 1:
+                parts = [group[len(group) // 2:], group[:len(group) // 2]]
+            for part in parts:
+                copies = scatter(part, step, residue)
+                if step == 0 and number == 0:
+                    for pieces, sends, gone, comes in edges:
+                        pl.when(sends)(gone.wait_send)
+                    all_in()
+                for copy in copies:
+                    copy.start()
 
         if step == 0:
             take_all(faces)
@@ -454,7 +477,7 @@
             g_high[...] = high.T
             g_low[...] = (propagator[...] - high.astype(f32)).astype(bf16).T
 
-        arrival(landed.at[step], r_send, r_recv.at[step]).wait_recv()
+        arrival(landed.at[step], r_send, r_recv[step]).wait_recv()
         parts = [kept[...]]
         each(lambda d, e: parts.append(landed[step, slot(d, e)].astype(f32)))
         summed = sum(parts[1:], parts[0])
@@ -484,7 +507,7 @@
     out_ref[...] = state
     reduced_sent()
     mine_sent()
-    for parts, sends, gone, comes in faces + edges:
+    for parts, sends, gone, comes in faces:
         pl.when(sends)(gone.wait_send)
     mate_gone.wait_send()
     mate_kappa.wait_send()
@@ -522,6 +545,7 @@
             pltpu.VMEM((3, samples), f32),
             pltpu.VMEM((wide, narrow, owned, modes), f32),
             pltpu.VMEM((modes, modes), f32),
+            pltpu.VMEM((modes // LANES, 2 * size_x + size_y, size_z, LANES), bf16),
             pltpu.VMEM((CORES, (2 * size_x + size_y) * size_z, narrow * unit), bf16),
             pltpu.VMEM((border * size_z, narrow * unit), bf16),
             pltpu.VMEM((border * size_z // LANES, narrow * unit, LANES), f32),
@@ -537,7 +561,7 @@
             pltpu.VMEM((owned, modes), f32),
             pltpu.VMEM((owned, modes), bf16),
             pltpu.VMEM((narrow, chips, owned, modes), bf16),
-            dma((5,)), dma((2,)), dma((4,)), dma((5,)), dma, dma((ITERS,)), dma, dma((narrow,)), dma((3,)), dma((4,)),
+            dma((5,)), dma((2,)), dma((4,)), dma((5,)), dma, dma((3,)), dma((max(4, narrow),)),
             pltpu.SemaphoreType.REGULAR((4 if chips > 2 else 2,)),
         ],
         compiler_params=pltpu.CompilerParams(

time: 23.9 us -> 24 us (level)
  no operation moved by 1% of the time
where the time goes in v4:
time: 24 us; the launch traced here: 23.9 us
  Pallas kernels  23.2 us (97%)
  local copies, waits for them, and re-layouts  0.62 us (3%)
    pallas_call x1, Pallas kernels, body(): pl.pallas_call(functools.partial(kernel, chips, narrow, scale), out_shape...  23.2 us
    unnamed x1, local copies, waits for them, and re-layouts  0.62 us

profile of v4, /device:TPU:0, one launch (start us, length us, event | category | flops | bytes accessed | tf_op | source)
XLA Modules:
  0.0 23.9 jit_solution(11792163678801667975)
XLA Ops:
  0.0 23.2 %shard_map.55 = f32[16,512]{1,0:T(8,128)S(1)} custom-call(bf16[16,16,2,512]{3,2,1,0:T(2,128)(2,1)} %basis_hbm.1, f32[16,2,16]{2,1,0:T(2,128)} %bitcast.3, f32[3,256]{1,0:T(4,128)} %velocity_hbm.1, f32[4,4,16,512]{3,2,1,0:T(8,128)} %bitcast.2, f32[512,512]{1,0:T(8,128)} %propagator_hbm.1), custom_call_target="tpu_custom_call" | custom-call | tf_op jit(solution)/shard_map/pallas_call | solution.py:536
  23.2 0.6 %copy.7 = f32[16,512]{1,0:T(8,128)} copy(f32[16,512]{1,0:T(8,128)S(1)} %shard_map.55) | data formatting | bytes 65536

commit v5 on v4

--- a/solution.py
+++ b/solution.py
@@ -422,8 +422,12 @@
         arrival(reduced, r_send, r_recv[0]).wait_send()
 
     def mine_sent():
-        arrival(reduced, g_send, r_recv[0]).wait_send()
-
+        count = narrow * chips - 1 - (chips - 1 if relayed else 0)
+        arrival(reduced.at[pl.ds(0, count)], g_send, r_recv[0]).wait_send()
+        if relayed:
+            arrival(reduced.at[pl.ds(0, chips - 1)], edge_send.at[2], r_recv[0]).wait_send()
+
+    relayed = far_n > 0 and chips > 1
     blocks_of = [[(d, e) for e in reversed(range(chips))] for d in range(narrow)]
     nearer, farther = range(narrow // 2), range(narrow // 2, narrow)
     if owned % 8 == 0:
@@ -431,7 +435,9 @@
         far_first.append(sum((blocks_of[d] for d in reversed(nearer)), []))
         near_first = [[(0, 0)], [(0, e) for e in range(1, chips)]]
         near_first += [blocks_of[d][::-1] for d in nearer if d > 0]
-        near_first.append(sum((blocks_of[d][::-1] for d in farther), []))
+        last = sum((blocks_of[d][::-1] for d in farther), [])
+        late = [(d, e) for d, e in last if relayed and d == far_n and e > 0]
+        near_first += [[block for block in last if block not in late], late]
         near_first = [group for group in near_first if group]
     else:
         far_first = [sum((blocks_of[d][::-1] for d in part), []) for part in (farther, nearer)]
@@ -442,6 +448,7 @@
             return [(d * chips + e) * owned + inner for d, e in group for inner in range(0, owned, 8)]
         return range(group[0][0] * unit, (group[-1][0] + 1) * unit, 8)
 
+    handing = max(4, narrow)
     state = coefficients[CORES * peer(chip, far_x) + core, peer(me_n, far_n)]
     residue = None
     for step in range(ITERS):
@@ -449,25 +456,32 @@
             reduced_sent()
         for number, group in enumerate(near_first if step else far_first):
             if step > 0:
-                for d in sorted({d for d, e in group if d > 0 or e > 0}):
-                    beyond = gathered.at[d] if d > 0 else gathered.at[0, pl.ds(1, chips - 1)]
-                    arrival(beyond, g_send, g_recv.at[d]).wait_recv()
+                for d in sorted({d for d, e in group if d + e > 0}):
+                    if relayed and d == far_n:
+                        if (d, 0) in group:
+                            arrival(gathered.at[d, 0], g_send, g_recv.at[d]).wait_recv()
+                            for e in range(1, chips):
+                                remote(
+                                    gathered.at[d, 0], gathered.at[d, e], edge_send.at[2], g_recv.at[handing],
+                                    CORES * peer(chip, e) + core, me_n,
+                                ).start()
+                        if (d, 1) in group:
+                            arrival(gathered.at[d, pl.ds(1, chips - 1)], g_send, g_recv.at[handing]).wait_recv()
+                    else:
+                        beyond = gathered.at[d] if d > 0 else gathered.at[0, pl.ds(1, chips - 1)]
+                        arrival(beyond, g_send, g_recv.at[d]).wait_recv()
                 rows = jnp.concatenate([gathered[d, e] if d + e > 0 else mine[...] for d, e in group], axis=0)
                 made = rounded(rows, slice(None))
                 for i, (d, e) in enumerate(group):
                     at = (d * chips + e) * owned
                     field[at:at + owned, :] = made[i * owned:(i + 1) * owned]
-            parts = [group]
-            if step > 0 and group is near_first[-1] and owned % 8 == 0 and len(group) > 1:
-                parts = [group[len(group) // 2:], group[:len(group) // 2]]
-            for part in parts:
-                copies = scatter(part, step, residue)
-                if step == 0 and number == 0:
-                    for pieces, sends, gone, comes in edges:
-                        pl.when(sends)(gone.wait_send)
-                    all_in()
-                for copy in copies:
-                    copy.start()
+            copies = scatter(group, step, residue)
+            if step == 0 and number == 0:
+                for pieces, sends, gone, comes in edges:
+                    pl.when(sends)(gone.wait_send)
+                all_in()
+            for copy in copies:
+                copy.start()
 
         if step == 0:
             take_all(faces)
@@ -498,7 +512,7 @@
             residue = state - state.astype(bf16).astype(f32)
             for d in [*reversed(nearer), *reversed(farther)]:
                 for e in reversed(range(chips)):
-                    if d + e > 0:
+                    if d + e > 0 and not (relayed and d == far_n and e > 0):
                         remote(
                             mine, gathered.at[d, e], g_send, g_recv.at[d],
                             CORES * peer(chip, e) + core, peer(me_n, d),
@@ -561,7 +575,7 @@
             pltpu.VMEM((owned, modes), f32),
             pltpu.VMEM((owned, modes), bf16),
             pltpu.VMEM((narrow, chips, owned, modes), bf16),
-            dma((5,)), dma((2,)), dma((4,)), dma((5,)), dma, dma((3,)), dma((max(4, narrow),)),
+            dma((5,)), dma((2,)), dma((4,)), dma((5,)), dma, dma((3,)), dma((max(4, narrow) + 1,)),
             pltpu.SemaphoreType.REGULAR((4 if chips > 2 else 2,)),
         ],
         compiler_params=pltpu.CompilerParams(

time: 24 us -> 23.9 us (level)
  no operation moved by 1% of the time
where the time goes in v5:
time: 23.9 us; the launch traced here: 23.8 us
  Pallas kernels  23.2 us (97%)
  local copies, waits for them, and re-layouts  0.62 us (3%)
    pallas_call x1, Pallas kernels, body(): pl.pallas_call(functools.partial(kernel, chips, narrow, scale), out_shape...  23.2 us
    unnamed x1, local copies, waits for them, and re-layouts  0.62 us

profile of v5, /device:TPU:0, one launch (start us, length us, event | category | flops | bytes accessed | tf_op | source)
XLA Modules:
  0.0 23.8 jit_solution(2741305711439802631)
XLA Ops:
  0.0 23.2 %shard_map.55 = f32[16,512]{1,0:T(8,128)S(1)} custom-call(bf16[16,16,2,512]{3,2,1,0:T(2,128)(2,1)} %basis_hbm.1, f32[16,2,16]{2,1,0:T(2,128)} %bitcast.3, f32[3,256]{1,0:T(4,128)} %velocity_hbm.1, f32[4,4,16,512]{3,2,1,0:T(8,128)} %bitcast.2, f32[512,512]{1,0:T(8,128)} %propagator_hbm.1), custom_call_target="tpu_custom_call" | custom-call | tf_op jit(solution)/shard_map/pallas_call | solution.py:550
  23.2 0.6 %copy.7 = f32[16,512]{1,0:T(8,128)} copy(f32[16,512]{1,0:T(8,128)S(1)} %shard_map.55) | data formatting | bytes 65536

commit v6 on v5

--- a/solution.py
+++ b/solution.py
@@ -431,8 +431,8 @@
     blocks_of = [[(d, e) for e in reversed(range(chips))] for d in range(narrow)]
     nearer, farther = range(narrow // 2), range(narrow // 2, narrow)
     if owned % 8 == 0:
-        far_first = [blocks_of[d] for d in reversed(farther)]
-        far_first.append(sum((blocks_of[d] for d in reversed(nearer)), []))
+        far_first = [blocks_of[narrow - 1], sum((blocks_of[d] for d in range(narrow - 2, 0, -1)), []), blocks_of[0]]
+        far_first = [group for group in far_first if group]
         near_first = [[(0, 0)], [(0, e) for e in range(1, chips)]]
         near_first += [blocks_of[d][::-1] for d in nearer if d > 0]
         last = sum((blocks_of[d][::-1] for d in farther), [])

time: 23.9 us -> 23.8 us (level)
  no operation moved by 1% of the time
where the time goes in v6:
time: 23.8 us; the launch traced here: 23.7 us
  Pallas kernels  23 us (97%)
  local copies, waits for them, and re-layouts  0.62 us (3%)
    pallas_call x1, Pallas kernels, body(): pl.pallas_call(functools.partial(kernel, chips, narrow, scale), out_shape...  23 us
    unnamed x1, local copies, waits for them, and re-layouts  0.62 us

profile of v6, /device:TPU:0, one launch (start us, length us, event | category | flops | bytes accessed | tf_op | source)
XLA Modules:
  0.0 23.7 jit_solution(671764829491501696)
XLA Ops:
  0.0 23.0 %shard_map.55 = f32[16,512]{1,0:T(8,128)S(1)} custom-call(bf16[16,16,2,512]{3,2,1,0:T(2,128)(2,1)} %basis_hbm.1, f32[16,2,16]{2,1,0:T(2,128)} %bitcast.3, f32[3,256]{1,0:T(4,128)} %velocity_hbm.1, f32[4,4,16,512]{3,2,1,0:T(8,128)} %bitcast.2, f32[512,512]{1,0:T(8,128)} %propagator_hbm.1), custom_call_target="tpu_custom_call" | custom-call | tf_op jit(solution)/shard_map/pallas_call | solution.py:550
  23.1 0.6 %copy.7 = f32[16,512]{1,0:T(8,128)} copy(f32[16,512]{1,0:T(8,128)S(1)} %shard_map.55) | data formatting | bytes 65536
